TPU v7x, 512 devices: a whole 4x4x16 slice. The times are simulated.
512 devices in a mesh: seq: 32 (over y, x, core), head: 16 (over z).
Axes of the slice: x: 4, y: 4, z: 16, core: 2. Of those that a mesh axis runs over, the one named last changes fastest.
Arguments:
- x_in: bfloat16 [8192, 8192], P('seq', 'head'), may hold values from -6 to 6
- b_in: bfloat16 [8192, 128], P(('seq', 'head')), may hold values from -0.5 to 0.5
- c_in: bfloat16 [8192, 128], P(('seq', 'head')), may hold values from -0.5 to 0.5
- decay_codes: int32 [128, 8192], P('head', 'seq'), may hold values from 0 to 7168
- decay_rate: float32 [128], P('head'), may hold values from 0 to 0.05
- skip_gain: float32 [128], P('head'), may hold values from 0.5 to 1.5
- out_grad: bfloat16 [8192, 8192], P('seq', 'head'), may hold values from -6 to 6
Outputs:
- ssm_out: bfloat16 [8192, 8192], P('seq', 'head')
- input_grad: bfloat16 [8192, 8192], P('seq', 'head')
- grad_b: float32 [8192, 128], P(('seq', 'head'))
- grad_c: float32 [8192, 128], P(('seq', 'head'))
All inputs are finite; a program needn't handle non-finite values.
Results may differ from a plain program's by a relative error of at most 0.005.
Values may be sent and summed in bfloat16 or wider, within the bound.
No kernel may reach another device: no remote copies, remote signals or barrier semaphores. Data moves between devices by JAX's collectives and lax.ppermute only.
A program may use at most 64 MiB of HBM per device.

v0:
```python
import jax
import jax.numpy as jnp
from jax import lax
from jax.sharding import PartitionSpec as P

HEAD_DIM = 64
STATE = 128
BLOCK = 256


def carried_in(x, axis, combine, identity, reverse):
    size, place = (lax.axis_size(axis), lax.axis_index(axis))
    everything = jax.tree.map(lambda part: lax.all_gather(part, axis), x)
    start = jax.tree.map(
        lambda part, zero: jnp.broadcast_to(jnp.asarray(zero, part.dtype), part.shape), x, identity
    )

    def hop(k, before):
        at = size - 1 - k if reverse else k
        reached = at > place if reverse else at < place
        new = combine(before, jax.tree.map(lambda part: part[at], everything))
        return jax.tree.map(lambda a, b: jnp.where(reached, a, b), new, before)

    return lax.fori_loop(0, size, hop, start)


def exact(form, operands):
    return jnp.einsum(form, *operands, precision=lax.Precision.HIGHEST)


def decode(decay_labels, decay_speeds):
    time_delta = 0.5 + (decay_labels % 1024).astype(jnp.float32) / 1024.0
    spike_loss_term = 0.1 * (decay_labels // 1024).astype(jnp.float32)
    return (time_delta, -decay_speeds[:, None] * time_delta - spike_loss_term)


def summarize(cumul, b_block, c_block, driven, cotangent):
    tail = jnp.exp(cumul[:, -1:] - cumul)
    state_part = exact("hj,jn,jhp->hpn", (tail, b_block.astype(jnp.float32), driven))
    adjoint_part = exact("hi,in,ihp->hpn", (jnp.exp(cumul), c_block.astype(jnp.float32), cotangent))
    return (state_part, adjoint_part)


def within(cumul, b_block, c_block, driven_low, cot_low):
    width = cumul.shape[1]
    causal = lax.broadcasted_iota(jnp.int32, (width, width), 0) >= lax.broadcasted_iota(
        jnp.int32, (width, width), 1
    )
    spread = cumul[:, :, None] - cumul[:, None, :]
    weights = jnp.where(causal, jnp.exp(jnp.where(causal, spread, 0.0)), 0.0)
    scores = jnp.dot(c_block, b_block.T, preferred_element_type=jnp.float32)
    mixed = (weights * scores).astype(jnp.bfloat16)
    out_part = jnp.einsum("hij,jhp->ihp", mixed, driven_low, preferred_element_type=jnp.float32)
    drive_grad = jnp.einsum("hij,ihp->jhp", mixed, cot_low, preferred_element_type=jnp.float32)
    pair_raw = jnp.einsum("ihp,jhp->hij", cot_low, driven_low, preferred_element_type=jnp.float32)
    paired = (weights * pair_raw).astype(jnp.bfloat16)
    c_grad = jnp.einsum("hij,jn->in", paired, b_block, preferred_element_type=jnp.float32)
    b_grad = jnp.einsum("hij,in->jn", paired, c_block, preferred_element_type=jnp.float32)
    return (out_part, drive_grad, c_grad, b_grad)


def summarize_group(group):
    return summarize(group[0], group[1], group[2], group[3], group[4])


def within_group(group):
    return within(group[0], group[1], group[2], group[5], group[6])


def both_group(group):
    return summarize_group(group) + within_group(group)


def link(before_part, after_part):
    return (
        before_part[0] + after_part[0],
        jnp.exp(after_part[0])[:, None, None] * before_part[1] + after_part[1],
    )


def advance(running, element):
    contrib, totals = element
    return (jnp.exp(totals)[:, None, None] * running + contrib, running)


def carries(state_parts, adjoint_parts, totals):
    head_count = totals.shape[1]
    blank_state = jnp.zeros(state_parts.shape[1:], jnp.float32)
    state_total, entering = lax.scan(advance, blank_state, (state_parts, totals))
    adjoint_total, outgoing_state = lax.scan(
        advance, blank_state, (adjoint_parts, totals), reverse=True
    )
    decay_total = jnp.sum(totals, axis=0)
    identity = (jnp.zeros((head_count,), jnp.float32), blank_state)
    state_in = carried_in((decay_total, state_total), "seq", link, identity, False)[1]
    adjoint_in = carried_in((decay_total, adjoint_total), "seq", link, identity, True)[1]
    running_sum = jnp.cumsum(totals, axis=0)
    before_sum = running_sum - totals
    after_sum = decay_total[None, :] - running_sum
    full_states = entering + jnp.exp(before_sum)[:, :, None, None] * state_in[None]
    full_adjoints = outgoing_state + jnp.exp(after_sum)[:, :, None, None] * adjoint_in[None]
    return (full_states, full_adjoints)


def local(x_in, b_in, c_in, decay_codes, decay_rate, skip_gain, out_grad):
    head_count = decay_rate.shape[0]
    token_count = x_in.shape[0]
    blocks = token_count // BLOCK
    b_full, output_matrix_full = (
        lax.all_gather(b_in, "head", axis=0, tiled=True),
        lax.all_gather(c_in, "head", axis=0, tiled=True),
    )
    time_delta, log_decay = decode(decay_codes, decay_rate)
    inputs = x_in.astype(jnp.float32).reshape(blocks, BLOCK, head_count, HEAD_DIM)
    cot_low = out_grad.reshape(blocks, BLOCK, head_count, HEAD_DIM)
    cotangent = cot_low.astype(jnp.float32)
    step_tokens = time_delta.reshape(head_count, blocks, BLOCK).transpose(1, 2, 0)[..., None]
    driven_low = (inputs * step_tokens).astype(jnp.bfloat16)
    driven = driven_low.astype(jnp.float32)
    cumul = jnp.cumsum(log_decay.reshape(head_count, blocks, BLOCK), axis=2).transpose(1, 0, 2)
    totals = cumul[:, :, -1]
    input_matrix_blocks = b_full.reshape(blocks, BLOCK, STATE)
    c_blocks = output_matrix_full.reshape(blocks, BLOCK, STATE)
    operands = (cumul, input_matrix_blocks, c_blocks, driven, cotangent, driven_low, cot_low)
    state_parts, adjoint_parts, out_part, drive_grad, c_grad, b_grad = lax.map(both_group, operands)
    full_states, full_adjoints = carries(state_parts, adjoint_parts, totals)
    growth = jnp.exp(cumul)
    tail = jnp.exp(totals[:, :, None] - cumul)
    c_wide = c_blocks.astype(jnp.float32)
    b_wide = input_matrix_blocks.astype(jnp.float32)
    out_cross = exact("khi,khpn,kin->kihp", (growth, full_states, c_wide))
    c_cross = exact("khi,kihp,khpn->kin", (growth, cotangent, full_states))
    drive_cross = exact("khj,khpn,kjn->kjhp", (tail, full_adjoints, b_wide))
    b_cross = exact("khj,kjhp,khpn->kjn", (tail, driven, full_adjoints))
    gain = skip_gain[None, None, :, None]
    ssm_out = (out_part + out_cross + gain * inputs).astype(jnp.bfloat16)
    ssm_out = ssm_out.reshape(token_count, head_count * HEAD_DIM)
    input_grad = (gain * cotangent + step_tokens * (drive_grad + drive_cross)).astype(jnp.bfloat16)
    input_grad = input_grad.reshape(token_count, head_count * HEAD_DIM)
    b_sum = (b_grad + b_cross).reshape(token_count, STATE)
    c_sum = (c_grad + c_cross).reshape(token_count, STATE)
    grad_b, grad_c = (
        lax.psum_scatter(b_sum, "head", scatter_dimension=0, tiled=True),
        lax.psum_scatter(c_sum, "head", scatter_dimension=0, tiled=True),
    )
    return (ssm_out, input_grad, grad_b, grad_c)


def solution(mesh):
    placed = (
        P("seq", "head"),
        P(("seq", "head"), None),
        P(("seq", "head"), None),
        P("head", "seq"),
        P("head"),
        P("head"),
        P("seq", "head"),
    )
    return jax.shard_map(
        local,
        mesh=mesh,
        in_specs=placed,
        out_specs=(
            P("seq", "head"),
            P("seq", "head"),
            P(("seq", "head"), None),
            P(("seq", "head"), None),
        ),
        check_vma=False,
    )
```

profile of v0, /device:TPU:2, one launch (start us, length us, event | category | flops | bytes accessed | tf_op | source)
XLA Modules:
  0.0 333.9 jit_solution(12462103326752002295)
XLA Ops:
  10.0 1.1 copy.50
  11.1 36.0 %all_gather.20 = bf16[256,128]{1,0:T(8,128)(2,1)S(1)} all-gather(bf16[16,128]{1,0:T(8,128)(2,1)} %param.13), channel_id=1, replica_groups=mesh['seq'=32,'head'=16] {'head'}, dimensions={0}, use_global_device_ids=true | all-gather | bytes 69632 | tf_op jit(solution)/shard_map/all_gather | solution.py:111
  47.1 1.1 convolution_add_fusion
  48.3 1.1 copy.43
  49.4 26.3 %all_gather.21 = bf16[256,128]{1,0:T(8,128)(2,1)S(1)} all-gather(bf16[16,128]{1,0:T(8,128)(2,1)S(1)} %copy-done), channel_id=1, replica_groups=mesh['seq'=32,'head'=16] {'head'}, dimensions={0}, use_global_device_ids=true | all-gather | bytes 69632 | tf_op jit(solution)/shard_map/all_gather | solution.py:110
  75.7 1.1 convolution_add_fusion.1
  76.9 21.6 %all-gather = f32[32,8,1]{1,2,0:T(1,128)S(1)} all-gather(f32[1,8,1]{1,2,0:T(1,128)S(1)} %copy.47), channel_id=2, replica_groups=mesh['seq'=32,'head'=16] {'seq'}, dimensions={0}, use_global_device_ids=true | all-gather | bytes 1056 | tf_op jit(solution)/shard_map/all_gather | solution.py:13
  99.6 12.9 %all-gather.8.cloned.1.call-done = f32[256,64,128]{2,1,0:T(8,128)} async-done(((f32[8,64,128]{2,1,0:T(8,128)}), f32[256,64,128]{2,1,0:T(8,128)}) %all-gather.8.cloned.1.call-update) | async-done | bytes 8388624 | tf_op jit(solution)/shard_map/all_gather | solution.py:13
  112.5 35.5 %while.21 = (s32[]{:T(128)}, f32[8,64,128]{2,1,0:T(8,128)S(1)}, s32[]{:T(128)}, f32[32,8]{1,0:T(8,128)S(1)}, f32[32,8,64,128]{3,2,1,0:T(8,128)}, /*index=5*/s32[]{:T(128)}, s32[]{:T(128)}, s32[]{:T(128)}, s32[]{:T(128)}) while((s32[]{:T(128)}, f32[8,64,128]{2,1,0:T(8,128)S(1)}, s32[]{:T(128)}, f32[32,8]{1,0:T(8,128)S(1)}, ...), condition=%wide.region_5.6_spmd.clone, body=%wide.region_4.5_spmd.clone.sunk | while | flops 262152 | bytes 786695 | solution.py:24
  112.5 1.1 fusion.53
  113.6 1.1 fusion.53
  114.7 1.1 fusion.53
  115.8 1.1 fusion.53
  116.9 1.1 fusion.53
  118.0 1.1 fusion.53
  119.2 1.1 fusion.53
  120.3 1.1 fusion.53
  121.4 1.1 fusion.53
  122.5 1.1 fusion.53
  123.6 1.1 fusion.53
  124.7 1.1 fusion.53
  125.8 1.1 fusion.53
  126.9 1.1 fusion.53
  128.0 1.1 fusion.53
  129.1 1.1 fusion.53
  130.2 1.1 fusion.53
  131.4 1.1 fusion.53
  132.5 1.1 fusion.53
  133.6 1.1 fusion.53
  134.7 1.1 fusion.53
  135.8 1.1 fusion.53
  136.9 1.1 fusion.53
  138.0 1.1 fusion.53
  139.1 1.1 fusion.53
  140.2 1.1 fusion.53
  141.4 1.1 fusion.53
  142.5 1.1 fusion.53
  143.6 1.1 fusion.53
  144.7 1.1 fusion.53
  145.8 1.1 fusion.53
  146.9 1.1 fusion.53
  150.3 33.8 %all-gather.6.cloned.1.call-done = f32[256,64,128]{2,1,0:T(8,128)} async-done(((f32[8,64,128]{2,1,0:T(8,128)}), f32[256,64,128]{2,1,0:T(8,128)}) %all-gather.6.cloned.1.call-update) | async-done | bytes 8388624 | tf_op jit(solution)/shard_map/all_gather | solution.py:13
  184.1 35.0 %while.20 = (s32[]{:T(128)}, f32[8,64,128]{2,1,0:T(8,128)S(1)}, s32[]{:T(128)}, f32[32,8]{1,0:T(8,128)S(1)}, f32[32,8,64,128]{3,2,1,0:T(8,128)}, /*index=5*/s32[]{:T(128)}, s32[]{:T(128)}) while((s32[]{:T(128)}, f32[8,64,128]{2,1,0:T(8,128)S(1)}, s32[]{:T(128)}, f32[32,8]{1,0:T(8,128)S(1)}, f32[32,8,64,128]{3,2,1,0:T(8,128)}, ...), condition=%wide.region_3.4_spmd.clone, body=%wide.region_2.3_spmd.clone.sunk | while | flops 262148 | bytes 786633 | solution.py:24
  185.2 1.1 fusion.52
  186.3 1.1 fusion.52
  187.4 1.1 fusion.52
  188.5 1.1 fusion.52
  192.9 1.1 fusion.52
  194.0 1.1 fusion.52
  195.1 1.1 fusion.52
  199.5 1.1 fusion.52
  200.6 1.1 fusion.52
  201.7 1.1 fusion.52
  202.8 1.1 fusion.52
  203.9 1.1 fusion.52
  205.0 1.1 fusion.52
  206.1 1.1 fusion.52
  209.3 1.1 fusion.52
  210.4 1.1 fusion.52
  212.6 1.1 fusion.52
  215.9 1.1 fusion.52
  217.0 1.1 fusion.52
  224.7 32.1 %reduce-scatter.3.cloned.1.call-done = f32[16,128]{1,0:T(8,128)} async-done(((f32[256,128]{1,0:T(8,128)}), f32[16,128]{1,0:T(8,128)}) %reduce-scatter.3.cloned.1.call-update) | async-done | bytes 8208 | tf_op jit(solution)/shard_map/reduce_scatter | solution.py:143
  256.8 70.5 %reduce-scatter.5.cloned.1.call-done = f32[16,128]{1,0:T(8,128)} async-done(((f32[256,128]{1,0:T(8,128)}), f32[16,128]{1,0:T(8,128)}) %reduce-scatter.5.cloned.1.call-update) | async-done | bytes 8208 | tf_op jit(solution)/shard_map/reduce_scatter | solution.py:144
  (117 shorter events, 26.3 us)
Async XLA Ops:
  7.2 42.2 %copy-start = (bf16[16,128]{1,0:T(8,128)(2,1)S(1)}, bf16[16,128]{1,0:T(8,128)(2,1)}, u32[]{:S(2)}) copy-start(bf16[16,128]{1,0:T(8,128)(2,1)} %param.12) | copy-start | bytes 12292
  7.2 105.3 %all-gather.8.cloned.1.call-start = ((), (), s32[]{:S(2)}) async-start(), calls=%async_computation.5 | async-start | bytes 8650752 | tf_op jit(solution)/shard_map/all_gather | solution.py:13
  48.2 135.9 %all-gather.6.cloned.1.call-start = ((), (), s32[]{:S(2)}) async-start(), calls=%async_computation.4 | async-start | bytes 8650752 | tf_op jit(solution)/shard_map/all_gather | solution.py:13
  76.8 180.0 %reduce-scatter.3.cloned.1.call-start = ((), (), s32[]{:S(2)}) async-start(), calls=%async_computation.2 | async-start | bytes 139264 | tf_op jit(solution)/shard_map/reduce_scatter | solution.py:143
  150.3 177.0 %reduce-scatter.5.cloned.1.call-start = ((), (), s32[]{:S(2)}) async-start(), calls=%async_computation.3 | async-start | bytes 139264 | tf_op jit(solution)/shard_map/reduce_scatter | solution.py:144
  184.1 36.1 %copy-start.1 = (f32[8]{0:T(128)S(1)}, f32[8]{0:T(128)}, u32[]{:S(2)}) copy-start(f32[8]{0:T(128)} %param.16) | copy-start | bytes 100
Sparse Core Ops, SparseCore 0:
  48.4 64.0 all-gather.7
  116.2 67.8 all-gather.5
  187.5 69.2 reduce-scatter.2
  260.0 67.2 reduce-scatter.4
where the time goes:
time: 336 us; the launch traced here: 334 us
  waiting for transfers between devices  149 us (44%)
  blocking collectives  83.9 us (25%)
  other arithmetic  69.9 us (21%)
  between operations  13.9 us (4%)
  matrix products  9.26 us (3%)
  local copies, waits for them, and re-layouts  5.13 us (2%)
    reduce_scatter x1, waiting for transfers between devices, local(): lax.psum_scatter(c_sum, 'head', scatter_dimension=0, tiled=True)  70.5 us
    select_n x64, other arithmetic, hop(): return jax.tree.map(lambda a, b: jnp.where(reached, a, b), new, before)  67.5 us
    all_gather x2, waiting for transfers between devices, carried_in(): everything = jax.tree.map(lambda part: lax.all_gather(part, axis), x)  46.7 us
    all_gather x1, blocking collectives, local(): lax.all_gather(c_in, 'head', axis=0, tiled=True)  36 us
    reduce_scatter x1, waiting for transfers between devices, local(): lax.psum_scatter(b_sum, 'head', scatter_dimension=0, tiled=True)  32.1 us
    all_gather x1, blocking collectives, local(): lax.all_gather(b_in, 'head', axis=0, tiled=True)  26.3 us
    all_gather x1, blocking collectives, carried_in(): everything = jax.tree.map(lambda part: lax.all_gather(part, axis), x)  21.6 us
  transfers between devices with their start and end apart: 4, of which 4 were waited for; matrix products, arithmetic and copies ran while one was open for 24% of the time, Pallas kernels for 0%

commit v1 on v0

v1 whole, which is shorter than its diff:
```python
import functools

import jax
import jax.numpy as jnp
from jax import lax
from jax.experimental import pallas as pl
from jax.experimental.pallas import tpu as pltpu
from jax.sharding import PartitionSpec as P

HEAD_DIM = 64
STATE = 128
BLOCK = 256
BF = jnp.bfloat16
F32 = jnp.float32


def dg(a, b, ca, cb):
    return lax.dot_general(a, b, (((ca,), (cb,)), ((), ())), preferred_element_type=F32)


def pieces(v, count):
    out = []
    for _ in range(count):
        part = v.astype(BF)
        out.append(part)
        v = v - part.astype(F32)
    return out


def split_dot(v, b, ca, cb):
    hi, lo = pieces(v, 2)
    return dg(hi, b, ca, cb) + dg(lo, b, ca, cb)


def spread_rows(rows, count):
    heads = rows.shape[0]
    stacked = jnp.concatenate([p.astype(F32) for p in pieces(rows, count)], axis=0).astype(BF)
    k = heads * count
    row = lax.broadcasted_iota(jnp.int32, (k, heads * HEAD_DIM), 0) % heads
    col = lax.broadcasted_iota(jnp.int32, (k, heads * HEAD_DIM), 1) // HEAD_DIM
    pick = jnp.where(row == col, 1.0, 0.0).astype(BF)
    return dg(stacked, pick, 0, 0)


def decode(codes, rate_ref):
    heads, tokens = codes.shape
    head = lax.broadcasted_iota(jnp.int32, (heads, tokens), 0)
    rate = jnp.zeros((heads, tokens), F32)
    for h in range(heads):
        rate = jnp.where(head == h, rate_ref[h], rate)
    delta = 0.5 + (codes & 1023).astype(F32) / 1024.0
    log_decay = -rate * delta - 0.1 * (codes >> 10).astype(F32)
    return delta, log_decay


def running_sum(log_decay):
    tokens = log_decay.shape[1]
    i = lax.broadcasted_iota(jnp.int32, (tokens, tokens), 0)
    j = lax.broadcasted_iota(jnp.int32, (tokens, tokens), 1)
    upper = jnp.where(i <= j, 1.0, 0.0).astype(BF)
    return sum(dg(p, upper, 1, 0) for p in pieces(log_decay, 3)[::-1])


def common(x_ref, dy_ref, codes_ref, rate_ref):
    delta, log_decay = decode(codes_ref[...], rate_ref)
    cumul = running_sum(log_decay)
    total = cumul[:, BLOCK - 1 :]
    growth = jnp.exp(cumul)
    tail = jnp.exp(total - cumul)
    delta_x = spread_rows(delta, 2)
    growth_x = spread_rows(growth, 3)
    tail_x = spread_rows(tail, 3)
    x = x_ref[...].astype(F32)
    dy = dy_ref[...].astype(F32)
    driven = (x * delta_x).astype(BF)
    return cumul, total, delta_x, growth_x, tail_x, x, dy, driven


def both(bc_ref):
    half = bc_ref.shape[1] // 2
    b = bc_ref[:, :half, :].reshape(BLOCK, STATE)
    c = bc_ref[:, half:, :].reshape(BLOCK, STATE)
    return b, c


def summary_kernel(bc_ref, x_ref, dy_ref, codes_ref, rate_ref, send_ref):
    b, c = both(bc_ref)
    _, total, _, growth_x, tail_x, _, dy, driven = common(x_ref, dy_ref, codes_ref, rate_ref)
    parts = send_ref.shape[0]
    state = split_dot(driven.astype(F32) * tail_x, b, 0, 0)
    adjoint = split_dot(dy * growth_x, c, 0, 0)
    send_ref[:, 0:16, :] = state.astype(BF).reshape(parts, 16, STATE)
    send_ref[:, 16:32, :] = adjoint.astype(BF).reshape(parts, 16, STATE)
    heads = total.shape[0]
    decay = jnp.exp(total)
    hi, mid, low = [p.astype(F32) for p in pieces(decay, 3)]
    row = lax.broadcasted_iota(jnp.int32, (8, STATE), 0)
    per = parts // heads
    for h in range(heads):
        tile = jnp.where(
            row == 0, hi[h : h + 1, :], jnp.where(row == 1, mid[h : h + 1, :], low[h : h + 1, :])
        ).astype(BF)
        for q in range(per):
            send_ref[h * per + q, 32:40, :] = tile


def scan_kernel(got_ref, send_ref):
    count = got_ref.shape[0]
    decays = []
    for k in range(count):
        tile = got_ref[k, 32:40, :].astype(F32)
        decays.append(tile[0:1] + tile[1:2] + tile[2:3])
    run = jnp.zeros((16, STATE), F32)
    for k in range(count):
        send_ref[k, 0:16, :] = run.astype(BF)
        run = decays[k] * run + got_ref[k, 0:16, :].astype(F32)
    run = jnp.zeros((16, STATE), F32)
    for k in reversed(range(count)):
        send_ref[k, 16:32, :] = run.astype(BF)
        run = decays[k] * run + got_ref[k, 16:32, :].astype(F32)


def finish_kernel(
    bc_ref, x_ref, dy_ref, codes_ref, rate_ref, gain_ref, in_ref, out_ref, grad_ref, sums_ref
):
    b, c = both(bc_ref)
    cumul, total, delta_x, growth_x, tail_x, x, dy, driven = common(
        x_ref, dy_ref, codes_ref, rate_ref
    )
    heads = total.shape[0]
    width = heads * HEAD_DIM
    i = lax.broadcasted_iota(jnp.int32, (BLOCK, BLOCK), 0)
    j = lax.broadcasted_iota(jnp.int32, (BLOCK, BLOCK), 1)
    causal = i >= j
    lower = jnp.where(causal, 1.0, 0.0).astype(BF)
    _, log_decay = decode(codes_ref[...], rate_ref)
    cumul_t = sum(dg(lower, p, 1, 1) for p in pieces(log_decay, 3)[::-1])
    scores = dg(c, b, 1, 1)
    low_dy = dy_ref[...]
    lane = lax.broadcasted_iota(jnp.int32, (BLOCK, 2 * HEAD_DIM), 1)
    first = lane < HEAD_DIM
    zero = jnp.zeros((BLOCK, 2 * HEAD_DIM), BF)
    paired = jnp.zeros((BLOCK, BLOCK), F32)
    outs, drives = [], []
    for pair in range(heads // 2):
        cut = slice(pair * 2 * HEAD_DIM, (pair + 1) * 2 * HEAD_DIM)
        u, g = driven[:, cut], low_dy[:, cut]
        made = []
        for side in range(2):
            h = 2 * pair + side
            spread = cumul_t[:, h : h + 1] - cumul[h : h + 1, :]
            weights = jnp.exp(jnp.where(causal, spread, -1e30))
            mixed = (weights * scores).astype(BF)
            own = first if side == 0 else jnp.logical_not(first)
            raw = dg(jnp.where(own, g, zero), u, 1, 1)
            paired = paired + (weights * raw).astype(BF).astype(F32)
            made.append((dg(mixed, u, 1, 0), dg(mixed, g, 0, 0)))
        outs.append(jnp.where(first, made[0][0], made[1][0]))
        drives.append(jnp.where(first, made[0][1], made[1][1]))
    out_part = jnp.concatenate(outs, axis=1)
    drive_grad = jnp.concatenate(drives, axis=1)
    state = in_ref[:, 0:16, :].reshape(width, STATE)
    adjoint = in_ref[:, 16:32, :].reshape(width, STATE)
    chan = lax.broadcasted_iota(jnp.int32, (1, width), 1) // HEAD_DIM
    gain = jnp.zeros((1, width), F32)
    for h in range(heads):
        gain = jnp.where(chan == h, gain_ref[h], gain)
    out_ref[...] = (out_part + growth_x * dg(c, state, 1, 1) + gain * x).astype(BF)
    grad_ref[...] = (
        gain * dy + delta_x * (drive_grad + tail_x * dg(b, adjoint, 1, 1))
    ).astype(BF)
    b_sum = split_dot(paired, c, 0, 0) + split_dot(driven.astype(F32) * tail_x, adjoint, 1, 0)
    c_sum = split_dot(paired, b, 1, 0) + split_dot(dy * growth_x, state, 1, 0)
    shape = sums_ref.shape[:2] + (STATE,)
    sums_ref[:, :, 0:STATE] = b_sum.astype(BF).reshape(shape)
    sums_ref[:, :, STATE:] = c_sum.astype(BF).reshape(shape)


def total_kernel(got_ref, b_ref, c_ref):
    acc = got_ref[0].astype(F32)
    for k in range(1, got_ref.shape[0]):
        acc = acc + got_ref[k].astype(F32)
    b_ref[...] = acc[:, 0:STATE]
    c_ref[...] = acc[:, STATE:]


VMEM = functools.partial(pl.BlockSpec, memory_space=pltpu.VMEM)
SMEM = functools.partial(pl.BlockSpec, memory_space=pltpu.SMEM)


def exchange(x, axis):
    return lax.all_to_all(x, axis, 0, 0, tiled=True)


def local(x_in, b_in, c_in, decay_codes, decay_rate, skip_gain, out_grad):
    seqs, groups = lax.axis_size("seq"), lax.axis_size("head")
    rows = b_in.shape[0]
    mine = jnp.concatenate([b_in, c_in], axis=0)
    bc = exchange(jnp.broadcast_to(mine[None], (groups, 2 * rows, STATE)), "head")
    send = pl.pallas_call(
        summary_kernel,
        out_shape=jax.ShapeDtypeStruct((seqs, 40, STATE), BF),
        in_specs=[VMEM(), VMEM(), VMEM(), VMEM(), SMEM()],
        out_specs=VMEM(),
        name="summary",
    )(bc, x_in, out_grad, decay_codes, decay_rate)
    got = exchange(send, "seq")
    back = pl.pallas_call(
        scan_kernel,
        out_shape=jax.ShapeDtypeStruct((seqs, 32, STATE), BF),
        in_specs=[VMEM()],
        out_specs=VMEM(),
        name="scan",
    )(got)
    carried = exchange(back, "seq")
    ssm_out, input_grad, sums = pl.pallas_call(
        finish_kernel,
        out_shape=(
            jax.ShapeDtypeStruct(x_in.shape, BF),
            jax.ShapeDtypeStruct(x_in.shape, BF),
            jax.ShapeDtypeStruct((groups, rows, 2 * STATE), BF),
        ),
        in_specs=[VMEM(), VMEM(), VMEM(), VMEM(), SMEM(), SMEM(), VMEM()],
        out_specs=(VMEM(), VMEM(), VMEM()),
        name="finish",
    )(bc, x_in, out_grad, decay_codes, decay_rate, skip_gain, carried)
    grad_b, grad_c = pl.pallas_call(
        total_kernel,
        out_shape=(jax.ShapeDtypeStruct((rows, STATE), F32),) * 2,
        in_specs=[VMEM()],
        out_specs=(VMEM(), VMEM()),
        name="total",
    )(exchange(sums, "head"))
    return ssm_out, input_grad, grad_b, grad_c


def solution(mesh):
    placed = (
        P("seq", "head"),
        P(("seq", "head"), None),
        P(("seq", "head"), None),
        P("head", "seq"),
        P("head"),
        P("head"),
        P("seq", "head"),
    )
    return jax.shard_map(
        local,
        mesh=mesh,
        in_specs=placed,
        out_specs=(
            P("seq", "head"),
            P("seq", "head"),
            P(("seq", "head"), None),
            P(("seq", "head"), None),
        ),
        check_vma=False,
    )
```

time: 336 us -> 91.4 us (0.27)
  the two profiles are of different devices: /device:TPU:2 before, /device:TPU:1 now
where the time goes in v1:
time: 91.4 us; the launch traced here: 90.3 us
  blocking collectives  78.2 us (86%)
  Pallas kernels  10.7 us (12%)
    all_to_all x4, blocking collectives, exchange(): return lax.all_to_all(x, axis, 0, 0, tiled=True)  78.2 us
    pallas_call x1, Pallas kernels, local(): pl.pallas_call(finish_kernel, out_shape=(jax.ShapeDtypeStruct(x_in.shape,...  4.48 us
    pallas_call x1, Pallas kernels, local(): pl.pallas_call(summary_kernel, out_shape=jax.ShapeDtypeStruct((seqs, 40,...  2.91 us

profile of v1, /device:TPU:1, one launch (start us, length us, event | category | flops | bytes accessed | tf_op | source)
XLA Modules:
  0.0 90.3 jit_solution(12879889382714578421)
XLA Ops:
  0.6 0.7 pad_maximum_fusion
  1.4 27.6 %all_to_all.20.bc_ref = bf16[16,32,128]{2,1,0:T(8,128)(2,1)} all-to-all(bf16[16,32,128]{2,1,0:T(8,128)(2,1)S(1)} %broadcast_in_dim.2), channel_id=1, replica_groups=mesh['seq'=32,'head'=16] {'head'}, dimensions={0} | all-to-all | bytes 262144 | tf_op jit(solution)/shard_map/all_to_all | solution.py:192
  29.0 2.9 %summary.1 = bf16[32,40,128]{2,1,0:T(8,128)(2,1)} custom-call(bf16[16,32,128]{2,1,0:T(8,128)(2,1)} %all_to_all.20.bc_ref, bf16[256,512]{1,0:T(8,128)(2,1)} %x_ref.3, bf16[256,512]{1,0:T(8,128)(2,1)} %dy_ref.3, s32[8,256]{1,0:T(8,128)} %codes_ref.3, f32[8]{0:T(128)} %rate_ref.3), custom_call_target="tpu_custom_call" | custom-call | tf_op jit(solution)/shard_map/summary/pallas_call | solution.py:200
  31.9 20.5 %all_to_all.21.got_ref = bf16[32,40,128]{2,1,0:T(8,128)(2,1)} all-to-all(bf16[32,40,128]{2,1,0:T(8,128)(2,1)} %summary.1), channel_id=1, replica_groups=mesh['seq'=32,'head'=16] {'seq'}, dimensions={0} | all-to-all | bytes 655360 | tf_op jit(solution)/shard_map/all_to_all | solution.py:192
  52.4 1.8 %scan.1 = bf16[32,32,128]{2,1,0:T(8,128)(2,1)} custom-call(bf16[32,40,128]{2,1,0:T(8,128)(2,1)} %all_to_all.21.got_ref), custom_call_target="tpu_custom_call" | custom-call | tf_op jit(solution)/shard_map/scan/pallas_call | solution.py:208
  54.1 13.4 %all_to_all.22.in_ref = bf16[32,32,128]{2,1,0:T(8,128)(2,1)} all-to-all(bf16[32,32,128]{2,1,0:T(8,128)(2,1)} %scan.1), channel_id=1, replica_groups=mesh['seq'=32,'head'=16] {'seq'}, dimensions={0} | all-to-all | bytes 524288 | tf_op jit(solution)/shard_map/all_to_all | solution.py:192
  67.5 4.5 %finish.1 = (bf16[256,512]{1,0:T(8,128)(2,1)}, bf16[256,512]{1,0:T(8,128)(2,1)}, bf16[16,16,256]{2,1,0:T(8,128)(2,1)}) custom-call(bf16[16,32,128]{2,1,0:T(8,128)(2,1)} %all_to_all.20.bc_ref, bf16[256,512]{1,0:T(8,128)(2,1)} %x_ref.3, bf16[256,512]{1,0:T(8,128)(2,1)} %dy_ref.3, s32[8,256]{1,0:T(8,128)} %codes_ref.3, f32[8]{0:T(128)} %rate_ref.3, f32[8]{0:T(128)} %gain_ref.1, ...), custom_call_target="tpu_custom_call" | custom-call | tf_op jit(solution)/shard_map/finish/pallas_call | solution.py:216
  72.0 16.8 %all_to_all.23.got_ref = bf16[16,16,256]{2,1,0:T(8,128)(2,1)} all-to-all(bf16[16,16,256]{2,1,0:T(8,128)(2,1)} %get-tuple-element.11), channel_id=1, replica_groups=mesh['seq'=32,'head'=16] {'head'}, dimensions={0} | all-to-all | bytes 262144 | tf_op jit(solution)/shard_map/all_to_all | solution.py:192
  88.8 1.5 %total.1 = (f32[16,128]{1,0:T(8,128)}, f32[16,128]{1,0:T(8,128)}) custom-call(bf16[16,16,256]{2,1,0:T(8,128)(2,1)} %all_to_all.23.got_ref), custom_call_target="tpu_custom_call" | custom-call | tf_op jit(solution)/shard_map/total/pallas_call | solution.py:227
  (1 shorter events, 0.0 us)

commit v2 on v1

v2 whole, which is shorter than its diff:
```python
import jax
import jax.numpy as jnp
from jax import lax
from jax.experimental import pallas as pl
from jax.experimental.pallas import tpu as pltpu
from jax.sharding import PartitionSpec as P

HEAD_DIM = 64
STATE = 128
BLOCK = 256
BF = jnp.bfloat16
F32 = jnp.float32


def dg(a, b, ca, cb):
    return lax.dot_general(a, b, (((ca,), (cb,)), ((), ())), preferred_element_type=F32)


def pieces(v, count):
    out = []
    for _ in range(count):
        part = v.astype(BF)
        out.append(part)
        v = v - part.astype(F32)
    return out


def split_dot(v, b, ca, cb):
    hi, lo = pieces(v, 2)
    return dg(hi, b, ca, cb) + dg(lo, b, ca, cb)


def stack(rows, count):
    return jnp.concatenate([p.astype(F32) for p in pieces(rows, count)], axis=0).astype(BF)


def expand(stacked, heads):
    shape = (stacked.shape[0], heads * HEAD_DIM)
    row = lax.broadcasted_iota(jnp.int32, shape, 0) % heads
    col = lax.broadcasted_iota(jnp.int32, shape, 1) // HEAD_DIM
    pick = jnp.where(row == col, 1.0, 0.0).astype(BF)
    return dg(stacked, pick, 0, 0)


def decode(codes, rate_ref):
    heads, tokens = codes.shape
    head = lax.broadcasted_iota(jnp.int32, (heads, tokens), 0)
    rate = jnp.zeros((heads, tokens), F32)
    for h in range(heads):
        rate = jnp.where(head == h, rate_ref[h], rate)
    delta = 0.5 + (codes & 1023).astype(F32) / 1024.0
    log_decay = -rate * delta - 0.1 * (codes >> 10).astype(F32)
    return delta, log_decay


def running_sum(log_decay):
    tokens = log_decay.shape[1]
    i = lax.broadcasted_iota(jnp.int32, (tokens, tokens), 0)
    j = lax.broadcasted_iota(jnp.int32, (tokens, tokens), 1)
    upper = jnp.where(i <= j, 1.0, 0.0).astype(BF)
    return sum(dg(p, upper, 1, 0) for p in pieces(log_decay, 3)[::-1])


def both(bc_ref):
    half = bc_ref.shape[1] // 2
    b = bc_ref[:, :half, :].reshape(BLOCK, STATE)
    c = bc_ref[:, half:, :].reshape(BLOCK, STATE)
    return b, c


def prepare_kernel(x_ref, dy_ref, codes_ref, rate_ref, td_ref, gd_ref, grow_ref, dt_ref, e_ref):
    delta, log_decay = decode(codes_ref[...], rate_ref)
    cumul = running_sum(log_decay)
    heads = delta.shape[0]
    total = cumul[:, BLOCK - 1 :]
    growth = stack(jnp.exp(cumul), 3)
    tail = jnp.exp(total - cumul)
    driven = (x_ref[...].astype(F32) * expand(stack(delta, 2), heads)).astype(BF)
    td_ref[0], td_ref[1] = pieces(driven.astype(F32) * expand(stack(tail, 3), heads), 2)
    gd_ref[0], gd_ref[1] = pieces(dy_ref[...].astype(F32) * expand(growth, heads), 2)
    grow_ref[...] = growth
    dt_ref[...] = stack(delta * tail, 3)
    hi, mid, low = [p.astype(F32) for p in pieces(jnp.exp(total), 3)]
    row = lax.broadcasted_iota(jnp.int32, (8, STATE), 0)
    for h in range(heads):
        e_ref[h] = jnp.where(
            row == 0, hi[h : h + 1, :], jnp.where(row == 1, mid[h : h + 1, :], low[h : h + 1, :])
        ).astype(BF)


def summary_kernel(bc_ref, td_ref, gd_ref, e_ref, send_ref):
    b, c = both(bc_ref)
    parts, heads = send_ref.shape[0], e_ref.shape[0]
    state = dg(td_ref[0], b, 0, 0) + dg(td_ref[1], b, 0, 0)
    adjoint = dg(gd_ref[0], c, 0, 0) + dg(gd_ref[1], c, 0, 0)
    send_ref[:, 0:16, :] = state.astype(BF).reshape(parts, 16, STATE)
    send_ref[:, 16:32, :] = adjoint.astype(BF).reshape(parts, 16, STATE)
    per = parts // heads
    for h in range(heads):
        for q in range(per):
            send_ref[h * per + q, 32:40, :] = e_ref[h]


def scan_kernel(got_ref, send_ref):
    count = got_ref.shape[0]
    decays = []
    for k in range(count):
        tile = got_ref[k, 32:40, :].astype(F32)
        decays.append(tile[0:1] + tile[1:2] + tile[2:3])
    run = jnp.zeros((16, STATE), F32)
    for k in range(count):
        send_ref[k, 0:16, :] = run.astype(BF)
        run = decays[k] * run + got_ref[k, 0:16, :].astype(F32)
    run = jnp.zeros((16, STATE), F32)
    for k in reversed(range(count)):
        send_ref[k, 16:32, :] = run.astype(BF)
        run = decays[k] * run + got_ref[k, 16:32, :].astype(F32)


def within_kernel(
    bc_ref, x_ref, dy_ref, codes_ref, rate_ref, gain_ref, out_ref, grad_ref, sums_ref
):
    b, c = both(bc_ref)
    delta, log_decay = decode(codes_ref[...], rate_ref)
    cumul = running_sum(log_decay)
    heads = cumul.shape[0]
    delta_x = expand(stack(delta, 2), heads)
    driven = (x_ref[...].astype(F32) * delta_x).astype(BF)
    i = lax.broadcasted_iota(jnp.int32, (BLOCK, BLOCK), 0)
    j = lax.broadcasted_iota(jnp.int32, (BLOCK, BLOCK), 1)
    causal = i >= j
    lower = jnp.where(causal, 1.0, 0.0).astype(BF)
    cumul_t = sum(dg(lower, p, 1, 1) for p in pieces(log_decay, 3)[::-1])
    scores = dg(c, b, 1, 1)
    lane = lax.broadcasted_iota(jnp.int32, (BLOCK, 2 * HEAD_DIM), 1)
    first = lane < HEAD_DIM
    zero = jnp.zeros((BLOCK, 2 * HEAD_DIM), BF)
    paired = jnp.zeros((BLOCK, BLOCK), F32)
    chan = lax.broadcasted_iota(jnp.int32, (1, 2 * HEAD_DIM), 1)
    for pair in range(heads // 2):
        cut = slice(pair * 2 * HEAD_DIM, (pair + 1) * 2 * HEAD_DIM)
        u, g = driven[:, cut], dy_ref[:, cut]
        made = []
        for side in range(2):
            h = 2 * pair + side
            spread = cumul_t[:, h : h + 1] - cumul[h : h + 1, :]
            weights = jnp.exp(jnp.where(causal, spread, -1e30))
            mixed = (weights * scores).astype(BF)
            own = first if side == 0 else jnp.logical_not(first)
            raw = dg(jnp.where(own, g, zero), u, 1, 1)
            paired = paired + (weights * raw).astype(BF).astype(F32)
            made.append((dg(mixed, u, 1, 0), dg(mixed, g, 0, 0)))
        gain = jnp.where(chan < HEAD_DIM, gain_ref[2 * pair], gain_ref[2 * pair + 1])
        out_ref[:, cut] = jnp.where(first, made[0][0], made[1][0]) + gain * x_ref[:, cut].astype(F32)
        grad_ref[:, cut] = (
            jnp.where(first, made[0][1], made[1][1]) * delta_x[:, cut] + gain * g.astype(F32)
        )
    sums_ref[:, 0:STATE] = split_dot(paired, c, 0, 0)
    sums_ref[:, STATE:] = split_dot(paired, b, 1, 0)


def finish_kernel(
    bc_ref, in_ref, out_in, grad_in, sums_in, td_ref, gd_ref, grow_ref, dt_ref, out_ref, grad_ref, sums_ref
):
    b, c = both(bc_ref)
    width = out_in.shape[1]
    heads = width // HEAD_DIM
    growth_x, scale_x = expand(grow_ref[...], heads), expand(dt_ref[...], heads)
    state = in_ref[:, 0:16, :].reshape(width, STATE)
    adjoint = in_ref[:, 16:32, :].reshape(width, STATE)
    shape = sums_ref.shape[:2] + (STATE,)
    b_sum = sums_in[:, 0:STATE] + dg(td_ref[0], adjoint, 1, 0) + dg(td_ref[1], adjoint, 1, 0)
    c_sum = sums_in[:, STATE:] + dg(gd_ref[0], state, 1, 0) + dg(gd_ref[1], state, 1, 0)
    sums_ref[:, :, 0:STATE] = b_sum.astype(BF).reshape(shape)
    sums_ref[:, :, STATE:] = c_sum.astype(BF).reshape(shape)
    out_ref[...] = (out_in[...] + growth_x * dg(c, state, 1, 1)).astype(BF)
    grad_ref[...] = (grad_in[...] + scale_x * dg(b, adjoint, 1, 1)).astype(BF)


def total_kernel(got_ref, b_ref, c_ref):
    acc = got_ref[0].astype(F32)
    for k in range(1, got_ref.shape[0]):
        acc = acc + got_ref[k].astype(F32)
    b_ref[...] = acc[:, 0:STATE]
    c_ref[...] = acc[:, STATE:]


def exchange(x, axis):
    return lax.all_to_all(x, axis, 0, 0, tiled=True)


def near(x):
    return pltpu.with_memory_space_constraint(x, pltpu.VMEM)


def kernel(body, name, outs, *args, scalars=(), far=(), kept=True):
    args = [x if i in scalars or i in far else near(x) for i, x in enumerate(args)]
    specs = [
        pl.BlockSpec(memory_space=pltpu.SMEM if i in scalars else pltpu.VMEM)
        for i in range(len(args))
    ]
    shapes = tuple(
        pltpu.VMEM(s, d) if kept else jax.ShapeDtypeStruct(s, d) for s, d in outs
    )
    got = pl.pallas_call(
        body,
        out_shape=shapes,
        in_specs=specs,
        out_specs=tuple(pl.BlockSpec(memory_space=pltpu.VMEM) for _ in outs),
        compiler_params=pltpu.CompilerParams(vmem_limit_bytes=16 << 20),
        name=name,
    )(*args)
    return got if len(outs) > 1 else got[0]


def local(x_in, b_in, c_in, decay_codes, decay_rate, skip_gain, out_grad):
    seqs, groups = lax.axis_size("seq"), lax.axis_size("head")
    rows = b_in.shape[0]
    heads, tokens = decay_codes.shape
    wide = x_in.shape
    mine = jnp.concatenate([b_in, c_in], axis=0)
    bc = exchange(jnp.broadcast_to(mine[None], (groups, 2 * rows, STATE)), "head")
    td, gd, grow, dt, e = kernel(
        prepare_kernel,
        "prepare",
        [
            ((2,) + wide, BF),
            ((2,) + wide, BF),
            ((3 * heads, tokens), BF),
            ((3 * heads, tokens), BF),
            ((heads, 8, STATE), BF),
        ],
        x_in,
        out_grad,
        decay_codes,
        decay_rate,
        scalars=(3,),
        far=(0, 1, 2),
    )
    send = kernel(summary_kernel, "summary", [((seqs, 40, STATE), BF)], bc, td, gd, e)
    got = exchange(send, "seq")
    out_part, grad_part, sums_part = kernel(
        within_kernel,
        "within",
        [(wide, F32), (wide, F32), ((tokens, 2 * STATE), F32)],
        bc,
        x_in,
        out_grad,
        decay_codes,
        decay_rate,
        skip_gain,
        scalars=(4, 5),
        far=(1, 2, 3),
    )
    back = kernel(scan_kernel, "scan", [((seqs, 32, STATE), BF)], got)
    carried = exchange(back, "seq")
    ssm_out, input_grad, sums = kernel(
        finish_kernel,
        "finish",
        [(wide, BF), (wide, BF), ((groups, rows, 2 * STATE), BF)],
        bc,
        carried,
        out_part,
        grad_part,
        sums_part,
        td,
        gd,
        grow,
        dt,
    )
    grad_b, grad_c = kernel(
        total_kernel,
        "total",
        [((rows, STATE), F32)] * 2,
        exchange(sums, "head"),
        kept=False,
    )
    return ssm_out, input_grad, grad_b, grad_c


def solution(mesh):
    placed = (
        P("seq", "head"),
        P(("seq", "head"), None),
        P(("seq", "head"), None),
        P("head", "seq"),
        P("head"),
        P("head"),
        P("seq", "head"),
    )
    return jax.shard_map(
        local,
        mesh=mesh,
        in_specs=placed,
        out_specs=(
            P("seq", "head"),
            P("seq", "head"),
            P(("seq", "head"), None),
            P(("seq", "head"), None),
        ),
        check_vma=False,
    )
```

time: 91.4 us -> 83.5 us (0.914)
  the two profiles are of different devices: /device:TPU:1 before, /device:TPU:32 now
where the time goes in v2:
time: 83.5 us; the launch traced here: 83 us
  waiting for transfers between devices  31.3 us (37%)
  starting transfers between devices  23.7 us (28%)
  blocking collectives  16.6 us (20%)
  Pallas kernels  6.91 us (8%)
  local copies, waits for them, and re-layouts  3.04 us (4%)
    all_to_all x3, waiting for transfers between devices, exchange(): return lax.all_to_all(x, axis, 0, 0, tiled=True)  31.3 us
    all_to_all x3, starting transfers between devices, exchange(): return lax.all_to_all(x, axis, 0, 0, tiled=True)  23.7 us
    all_to_all x1, blocking collectives, exchange(): return lax.all_to_all(x, axis, 0, 0, tiled=True)  16.6 us
    pallas_call x6, Pallas kernels, kernel(): pl.pallas_call(body, out_shape=shapes, in_specs=specs, out_specs=tuple((p...  6.91 us
    unnamed x12, local copies, waits for them, and re-layouts  2.36 us
  transfers between devices with their start and end apart: 3, of which 3 were waited for; matrix products, arithmetic and copies ran while one was open for 2% of the time, Pallas kernels for 4%

profile of v2, /device:TPU:32, one launch (start us, length us, event | category | flops | bytes accessed | tf_op | source)
XLA Modules:
  0.0 83.0 jit_solution(12276300438790628926)
XLA Ops:
  0.6 0.0 copy-start
  0.6 0.7 pad_maximum_fusion
  1.4 0.7 broadcast_in_dim.2
  2.1 0.0 copy-start.2
  2.1 0.0 copy-start.3
  2.1 15.3 %all-to-all-start = ((bf16[16,32,128]{2,1,0:T(8,128)(2,1)}), bf16[16,32,128]{2,1,0:T(8,128)(2,1)S(1)}, u32[]{:S(2)}, u32[]{:S(2)}) async-start(bf16[16,32,128]{2,1,0:T(8,128)(2,1)} %broadcast_in_dim.2), calls=%async_computation | async-start | bytes 262144 | tf_op jit(solution)/shard_map/all_to_all | solution.py:189
  17.4 0.0 copy-done
  17.4 0.0 copy-done.2
  17.4 0.0 copy-done.3
  17.4 0.0 copy-start.1
  17.4 0.9 %copy-done.1 = bf16[256,512]{1,0:T(8,128)(2,1)S(1)} copy-done((bf16[256,512]{1,0:T(8,128)(2,1)S(1)}, bf16[256,512]{1,0:T(8,128)(2,1)}, u32[]{:S(2)}) %copy-start.1) | copy-done | bytes 262168
  18.4 1.2 %prepare.1 = (bf16[2,256,512]{2,1,0:T(8,128)(2,1)S(1)}, bf16[2,256,512]{2,1,0:T(8,128)(2,1)S(1)}, bf16[24,256]{1,0:T(8,128)(2,1)S(1)}, bf16[24,256]{1,0:T(8,128)(2,1)S(1)}, bf16[8,8,128]{2,1,0:T(8,128)(2,1)S(1)}) custom-call(bf16[256,512]{1,0:T(8,128)(2,1)S(1)} %copy-done, bf16[256,512]{1,0:T(8,128)(2,1)S(1)} %copy-done.1, s32[8,256]{1,0:T(8,128)S(1)} %copy-done.2, ...), custom_call_target="tpu_custom_call" | custom-call | tf_op jit(solution)/shard_map/prepare/pallas_call | solution.py:205
  19.6 12.0 %all-to-all-done.bc_ref = bf16[16,32,128]{2,1,0:T(8,128)(2,1)S(1)} async-done(((bf16[16,32,128]{2,1,0:T(8,128)(2,1)}), bf16[16,32,128]{2,1,0:T(8,128)(2,1)S(1)}, u32[]{:S(2)}, u32[]{:S(2)}) %all-to-all-start) | async-done | bytes 131104 | tf_op jit(solution)/shard_map/all_to_all | solution.py:189
  31.6 0.5 summary.1
  32.1 16.6 %all_to_all.20.got_ref = bf16[32,40,128]{2,1,0:T(8,128)(2,1)S(1)} all-to-all(bf16[32,40,128]{2,1,0:T(8,128)(2,1)S(1)} %summary.1), channel_id=1, replica_groups=mesh['seq'=32,'head'=16] {'seq'}, dimensions={0} | all-to-all | bytes 655360 | tf_op jit(solution)/shard_map/all_to_all | solution.py:189
  48.7 0.8 scan.1
  49.5 0.0 copy-start.4
  49.6 4.0 %all-to-all-start.2 = ((bf16[32,32,128]{2,1,0:T(8,128)(2,1)}), bf16[32,32,128]{2,1,0:T(8,128)(2,1)S(1)}, u32[]{:S(2)}, u32[]{:S(2)}) async-start(bf16[32,32,128]{2,1,0:T(8,128)(2,1)} %scan.1), calls=%async_computation.2 | async-start | bytes 524288 | tf_op jit(solution)/shard_map/all_to_all | solution.py:189
  53.6 0.0 copy-done.4
  53.6 2.4 %within.1 = (f32[256,512]{1,0:T(8,128)S(1)}, f32[256,512]{1,0:T(8,128)S(1)}, f32[256,256]{1,0:T(8,128)S(1)}) custom-call(bf16[16,32,128]{2,1,0:T(8,128)(2,1)S(1)} %all-to-all-done.bc_ref, bf16[256,512]{1,0:T(8,128)(2,1)S(1)} %copy-done, bf16[256,512]{1,0:T(8,128)(2,1)S(1)} %copy-done.1, s32[8,256]{1,0:T(8,128)S(1)} %copy-done.2, f32[8]{0:T(128)S(1)} %copy-done.3, ...), custom_call_target="tpu_custom_call" | custom-call | tf_op jit(solution)/shard_map/within/pallas_call | solution.py:205
  56.0 6.3 %all-to-all-done.2.in_ref = bf16[32,32,128]{2,1,0:T(8,128)(2,1)S(1)} async-done(((bf16[32,32,128]{2,1,0:T(8,128)(2,1)}), bf16[32,32,128]{2,1,0:T(8,128)(2,1)S(1)}, u32[]{:S(2)}, u32[]{:S(2)}) %all-to-all-start.2) | async-done | bytes 262176 | tf_op jit(solution)/shard_map/all_to_all | solution.py:189
  62.3 1.3 %finish.1 = (bf16[256,512]{1,0:T(8,128)(2,1)S(1)}, bf16[256,512]{1,0:T(8,128)(2,1)S(1)}, bf16[16,16,256]{2,1,0:T(8,128)(2,1)}) custom-call(bf16[16,32,128]{2,1,0:T(8,128)(2,1)S(1)} %all-to-all-done.bc_ref, bf16[32,32,128]{2,1,0:T(8,128)(2,1)S(1)} %all-to-all-done.2.in_ref, f32[256,512]{1,0:T(8,128)S(1)} %get-tuple-element.20.out_in, ...), custom_call_target="tpu_custom_call" | custom-call | tf_op jit(solution)/shard_map/finish/pallas_call | solution.py:205
  63.7 4.3 %all-to-all-start.3 = ((bf16[16,16,256]{2,1,0:T(8,128)(2,1)}), bf16[16,16,256]{2,1,0:T(8,128)(2,1)S(1)}, u32[]{:S(2)}, u32[]{:S(2)}) async-start(bf16[16,16,256]{2,1,0:T(8,128)(2,1)} %get-tuple-element.27), calls=%async_computation.3 | async-start | bytes 262144 | tf_op jit(solution)/shard_map/all_to_all | solution.py:189
  68.0 0.7 copy.11
  68.7 0.7 copy.12
  69.4 13.0 %all-to-all-done.3.got_ref = bf16[16,16,256]{2,1,0:T(8,128)(2,1)S(1)} async-done(((bf16[16,16,256]{2,1,0:T(8,128)(2,1)}), bf16[16,16,256]{2,1,0:T(8,128)(2,1)S(1)}, u32[]{:S(2)}, u32[]{:S(2)}) %all-to-all-start.3) | async-done | bytes 131104 | tf_op jit(solution)/shard_map/all_to_all | solution.py:189
  82.4 0.6 total.1
Async XLA Ops:
  0.6 16.8 %copy-start = (bf16[256,512]{1,0:T(8,128)(2,1)S(1)}, bf16[256,512]{1,0:T(8,128)(2,1)}, u32[]{:S(2)}) copy-start(bf16[256,512]{1,0:T(8,128)(2,1)} %x_ref.3) | copy-start | bytes 786436
  2.1 15.4 %copy-start.2 = (s32[8,256]{1,0:T(8,128)S(1)}, s32[8,256]{1,0:T(8,128)}, u32[]{:S(2)}) copy-start(s32[8,256]{1,0:T(8,128)} %codes_ref.3) | copy-start | bytes 24580
  2.1 15.4 %copy-start.3 = (f32[8]{0:T(128)S(1)}, f32[8]{0:T(128)}, u32[]{:S(2)}) copy-start(f32[8]{0:T(128)} %rate_ref.3) | copy-start | bytes 100
  2.1 29.6 %all-to-all-start = ((bf16[16,32,128]{2,1,0:T(8,128)(2,1)}), bf16[16,32,128]{2,1,0:T(8,128)(2,1)S(1)}, u32[]{:S(2)}, u32[]{:S(2)}) async-start(bf16[16,32,128]{2,1,0:T(8,128)(2,1)} %broadcast_in_dim.2), calls=%async_computation | async-start | bytes 262144 | tf_op jit(solution)/shard_map/all_to_all | solution.py:189
  17.4 1.0 %copy-start.1 = (bf16[256,512]{1,0:T(8,128)(2,1)S(1)}, bf16[256,512]{1,0:T(8,128)(2,1)}, u32[]{:S(2)}) copy-start(bf16[256,512]{1,0:T(8,128)(2,1)} %dy_ref.3) | copy-start | bytes 786436
  49.5 4.0 %copy-start.4 = (f32[8]{0:T(128)S(1)}, f32[8]{0:T(128)}, u32[]{:S(2)}) copy-start(f32[8]{0:T(128)} %gain_ref.1) | copy-start | bytes 100
  49.6 12.8 %all-to-all-start.2 = ((bf16[32,32,128]{2,1,0:T(8,128)(2,1)}), bf16[32,32,128]{2,1,0:T(8,128)(2,1)S(1)}, u32[]{:S(2)}, u32[]{:S(2)}) async-start(bf16[32,32,128]{2,1,0:T(8,128)(2,1)} %scan.1), calls=%async_computation.2 | async-start | bytes 524288 | tf_op jit(solution)/shard_map/all_to_all | solution.py:189
  63.7 18.7 %all-to-all-start.3 = ((bf16[16,16,256]{2,1,0:T(8,128)(2,1)}), bf16[16,16,256]{2,1,0:T(8,128)(2,1)S(1)}, u32[]{:S(2)}, u32[]{:S(2)}) async-start(bf16[16,16,256]{2,1,0:T(8,128)(2,1)} %get-tuple-element.27), calls=%async_computation.3 | async-start | bytes 262144 | tf_op jit(solution)/shard_map/all_to_all | solution.py:189

commit v3 on v2

--- a/solution.py
+++ b/solution.py
@@ -10,6 +10,13 @@
 BLOCK = 256
 BF = jnp.bfloat16
 F32 = jnp.float32
+HEAD_START = 8
+SEQ_START = 20
+
+
+def turned(count, start):
+    start = start if start < count else 0
+    return [(k + start) % count for k in range(count)]
 
 
 def dg(a, b, ca, cb):
@@ -62,9 +69,12 @@
 
 
 def both(bc_ref):
-    half = bc_ref.shape[1] // 2
-    b = bc_ref[:, :half, :].reshape(BLOCK, STATE)
-    c = bc_ref[:, half:, :].reshape(BLOCK, STATE)
+    groups, half = bc_ref.shape[0], bc_ref.shape[1] // 2
+    order = turned(groups, HEAD_START)
+    b, c = [
+        jnp.concatenate([bc_ref[order.index(g), rows, :] for g in range(groups)], axis=0)
+        for rows in (slice(0, half), slice(half, 2 * half))
+    ]
     return b, c
 
 
@@ -103,16 +113,18 @@
 
 def scan_kernel(got_ref, send_ref):
     count = got_ref.shape[0]
-    decays = []
-    for k in range(count):
+    order = turned(count, SEQ_START)
+    slots = [order.index(k) for k in range(count)]
+    decays = {}
+    for k in slots:
         tile = got_ref[k, 32:40, :].astype(F32)
-        decays.append(tile[0:1] + tile[1:2] + tile[2:3])
+        decays[k] = tile[0:1] + tile[1:2] + tile[2:3]
     run = jnp.zeros((16, STATE), F32)
-    for k in range(count):
+    for k in slots:
         send_ref[k, 0:16, :] = run.astype(BF)
         run = decays[k] * run + got_ref[k, 0:16, :].astype(F32)
     run = jnp.zeros((16, STATE), F32)
-    for k in reversed(range(count)):
+    for k in slots[::-1]:
         send_ref[k, 16:32, :] = run.astype(BF)
         run = decays[k] * run + got_ref[k, 16:32, :].astype(F32)
 
@@ -159,22 +171,26 @@
     sums_ref[:, STATE:] = split_dot(paired, b, 1, 0)
 
 
-def finish_kernel(
-    bc_ref, in_ref, out_in, grad_in, sums_in, td_ref, gd_ref, grow_ref, dt_ref, out_ref, grad_ref, sums_ref
-):
+def sums_kernel(in_ref, sums_in, td_ref, gd_ref, sums_ref):
+    width = td_ref.shape[2]
+    state = in_ref[:, 0:16, :].reshape(width, STATE)
+    adjoint = in_ref[:, 16:32, :].reshape(width, STATE)
+    groups, rows = sums_ref.shape[:2]
+    b_sum = sums_in[:, 0:STATE] + dg(td_ref[0], adjoint, 1, 0) + dg(td_ref[1], adjoint, 1, 0)
+    c_sum = sums_in[:, STATE:] + dg(gd_ref[0], state, 1, 0) + dg(gd_ref[1], state, 1, 0)
+    for slot, g in enumerate(turned(groups, HEAD_START)):
+        sums_ref[slot, :, 0:STATE] = b_sum[g * rows : (g + 1) * rows].astype(BF)
+        sums_ref[slot, :, STATE:] = c_sum[g * rows : (g + 1) * rows].astype(BF)
+
+
+def finish_kernel(bc_ref, in_ref, out_in, grad_in, grow_ref, dt_ref, out_ref, grad_ref):
     b, c = both(bc_ref)
     width = out_in.shape[1]
     heads = width // HEAD_DIM
-    growth_x, scale_x = expand(grow_ref[...], heads), expand(dt_ref[...], heads)
     state = in_ref[:, 0:16, :].reshape(width, STATE)
     adjoint = in_ref[:, 16:32, :].reshape(width, STATE)
-    shape = sums_ref.shape[:2] + (STATE,)
-    b_sum = sums_in[:, 0:STATE] + dg(td_ref[0], adjoint, 1, 0) + dg(td_ref[1], adjoint, 1, 0)
-    c_sum = sums_in[:, STATE:] + dg(gd_ref[0], state, 1, 0) + dg(gd_ref[1], state, 1, 0)
-    sums_ref[:, :, 0:STATE] = b_sum.astype(BF).reshape(shape)
-    sums_ref[:, :, STATE:] = c_sum.astype(BF).reshape(shape)
-    out_ref[...] = (out_in[...] + growth_x * dg(c, state, 1, 1)).astype(BF)
-    grad_ref[...] = (grad_in[...] + scale_x * dg(b, adjoint, 1, 1)).astype(BF)
+    out_ref[...] = (out_in[...] + expand(grow_ref[...], heads) * dg(c, state, 1, 1)).astype(BF)
+    grad_ref[...] = (grad_in[...] + expand(dt_ref[...], heads) * dg(b, adjoint, 1, 1)).astype(BF)
 
 
 def total_kernel(got_ref, b_ref, c_ref):
@@ -186,7 +202,9 @@
 
 
 def exchange(x, axis):
-    return lax.all_to_all(x, axis, 0, 0, tiled=True)
+    count = lax.axis_size(axis)
+    order = turned(count, HEAD_START if axis == "head" else SEQ_START)
+    return lax.all_to_all(x, axis, 0, 0, tiled=True, axis_index_groups=[order])
 
 
 def near(x):
@@ -254,26 +272,23 @@
     )
     back = kernel(scan_kernel, "scan", [((seqs, 32, STATE), BF)], got)
     carried = exchange(back, "seq")
-    ssm_out, input_grad, sums = kernel(
+    sums = kernel(
+        sums_kernel, "sums", [((groups, rows, 2 * STATE), BF)], carried, sums_part, td, gd
+    )
+    totals = exchange(sums, "head")
+    ssm_out, input_grad = kernel(
         finish_kernel,
         "finish",
-        [(wide, BF), (wide, BF), ((groups, rows, 2 * STATE), BF)],
+        [(wide, BF), (wide, BF)],
         bc,
         carried,
         out_part,
         grad_part,
-        sums_part,
-        td,
-        gd,
         grow,
         dt,
     )
     grad_b, grad_c = kernel(
-        total_kernel,
-        "total",
-        [((rows, STATE), F32)] * 2,
-        exchange(sums, "head"),
-        kept=False,
+        total_kernel, "total", [((rows, STATE), F32)] * 2, totals, kept=False
     )
     return ssm_out, input_grad, grad_b, grad_c
 

time: 83.5 us -> 76.3 us (0.914)
  the two profiles are of different devices: /device:TPU:32 before, /device:TPU:1 now
where the time goes in v3:
time: 76.3 us; the launch traced here: 75.8 us
  starting transfers between devices  38.9 us (51%)
  blocking collectives  14.5 us (19%)
  waiting for transfers between devices  10.8 us (14%)
  Pallas kernels  7.11 us (9%)
  local copies, waits for them, and re-layouts  3.05 us (4%)
    all_to_all x3, starting transfers between devices, exchange(): return lax.all_to_all(x, axis, 0, 0, tiled=True, axis_index_groups=[order])  38.9 us
    all_to_all x1, blocking collectives, exchange(): return lax.all_to_all(x, axis, 0, 0, tiled=True, axis_index_groups=[order])  14.5 us
    all_to_all x3, waiting for transfers between devices, exchange(): return lax.all_to_all(x, axis, 0, 0, tiled=True, axis_index_groups=[order])  10.8 us
    pallas_call x7, Pallas kernels, kernel(): pl.pallas_call(body, out_shape=shapes, in_specs=specs, out_specs=tuple((p...  7.11 us
    unnamed x14, local copies, waits for them, and re-layouts  2.37 us
  transfers between devices with their start and end apart: 3, of which 3 were waited for; matrix products, arithmetic and copies ran while one was open for 2% of the time, Pallas kernels for 5%

profile of v3, /device:TPU:1, one launch (start us, length us, event | category | flops | bytes accessed | tf_op | source)
XLA Modules:
  0.0 75.8 jit_solution(12032275152412610596)
XLA Ops:
  0.6 0.0 copy-start
  0.6 0.7 pad_maximum_fusion
  1.4 0.7 broadcast_in_dim.2
  2.1 0.0 copy-start.3
  2.1 0.0 copy-start.4
  2.1 19.2 %all-to-all-start = ((bf16[16,32,128]{2,1,0:T(8,128)(2,1)}), bf16[16,32,128]{2,1,0:T(8,128)(2,1)S(1)}, u32[]{:S(2)}, u32[]{:S(2)}) async-start(bf16[16,32,128]{2,1,0:T(8,128)(2,1)} %broadcast_in_dim.2), calls=%async_computation | async-start | bytes 262144 | tf_op jit(solution)/shard_map/all_to_all | solution.py:207
  21.3 0.0 copy-done
  21.3 0.0 copy-done.3
  21.3 0.0 copy-done.4
  21.3 0.0 copy-start.1
  21.3 0.9 %copy-done.1 = bf16[256,512]{1,0:T(8,128)(2,1)S(1)} copy-done((bf16[256,512]{1,0:T(8,128)(2,1)S(1)}, bf16[256,512]{1,0:T(8,128)(2,1)}, u32[]{:S(2)}) %copy-start.1) | copy-done | bytes 262168
  22.3 1.2 %prepare.1 = (bf16[2,256,512]{2,1,0:T(8,128)(2,1)S(1)}, bf16[2,256,512]{2,1,0:T(8,128)(2,1)S(1)}, bf16[24,256]{1,0:T(8,128)(2,1)S(1)}, bf16[24,256]{1,0:T(8,128)(2,1)S(1)}, bf16[8,8,128]{2,1,0:T(8,128)(2,1)S(1)}) custom-call(bf16[256,512]{1,0:T(8,128)(2,1)S(1)} %copy-done, bf16[256,512]{1,0:T(8,128)(2,1)S(1)} %copy-done.1, s32[8,256]{1,0:T(8,128)S(1)} %copy-done.3, ...), custom_call_target="tpu_custom_call" | custom-call | tf_op jit(solution)/shard_map/prepare/pallas_call | solution.py:223
  23.5 4.3 %all-to-all-done.bc_ref = bf16[16,32,128]{2,1,0:T(8,128)(2,1)S(1)} async-done(((bf16[16,32,128]{2,1,0:T(8,128)(2,1)}), bf16[16,32,128]{2,1,0:T(8,128)(2,1)S(1)}, u32[]{:S(2)}, u32[]{:S(2)}) %all-to-all-start) | async-done | bytes 131104 | tf_op jit(solution)/shard_map/all_to_all | solution.py:207
  27.8 0.5 summary.1
  28.3 14.5 %all_to_all.20.got_ref = bf16[32,40,128]{2,1,0:T(8,128)(2,1)S(1)} all-to-all(bf16[32,40,128]{2,1,0:T(8,128)(2,1)S(1)} %summary.1), channel_id=1, replica_groups={{320,336,352,368,384,400,416,432,448,464,480,496,0,16,32,48,64,80,96,11..., dimensions={0} | all-to-all | bytes 655360 | tf_op jit(solution)/shard_map/all_to_all | solution.py:207
  42.8 0.8 %scan.1 = bf16[32,32,128]{2,1,0:T(8,128)(2,1)} custom-call(bf16[32,40,128]{2,1,0:T(8,128)(2,1)S(1)} %all_to_all.20.got_ref), custom_call_target="tpu_custom_call" | custom-call | tf_op jit(solution)/shard_map/scan/pallas_call | solution.py:223
  43.6 0.0 copy-start.2
  43.6 0.0 copy-start.5
  43.6 8.2 %all-to-all-start.2 = ((bf16[32,32,128]{2,1,0:T(8,128)(2,1)}), bf16[32,32,128]{2,1,0:T(8,128)(2,1)S(1)}, u32[]{:S(2)}, u32[]{:S(2)}) async-start(bf16[32,32,128]{2,1,0:T(8,128)(2,1)} %scan.1), calls=%async_computation.2 | async-start | bytes 524288 | tf_op jit(solution)/shard_map/all_to_all | solution.py:207
  51.8 0.0 copy-done.2
  51.8 0.0 copy-done.5
  51.8 2.4 %within.1 = (f32[256,512]{1,0:T(8,128)S(1)}, f32[256,512]{1,0:T(8,128)S(1)}, f32[256,256]{1,0:T(8,128)S(1)}) custom-call(bf16[16,32,128]{2,1,0:T(8,128)(2,1)S(1)} %all-to-all-done.bc_ref, bf16[256,512]{1,0:T(8,128)(2,1)S(1)} %copy-done, bf16[256,512]{1,0:T(8,128)(2,1)S(1)} %copy-done.2, s32[8,256]{1,0:T(8,128)S(1)} %copy-done.3, f32[8]{0:T(128)S(1)} %copy-done.4, ...), custom_call_target="tpu_custom_call" | custom-call | tf_op jit(solution)/shard_map/within/pallas_call | solution.py:223
  54.3 1.7 %all-to-all-done.2.in_ref = bf16[32,32,128]{2,1,0:T(8,128)(2,1)S(1)} async-done(((bf16[32,32,128]{2,1,0:T(8,128)(2,1)}), bf16[32,32,128]{2,1,0:T(8,128)(2,1)S(1)}, u32[]{:S(2)}, u32[]{:S(2)}) %all-to-all-start.2) | async-done | bytes 262176 | tf_op jit(solution)/shard_map/all_to_all | solution.py:207
  55.9 1.1 %sums.1 = bf16[16,16,256]{2,1,0:T(8,128)(2,1)} custom-call(bf16[32,32,128]{2,1,0:T(8,128)(2,1)S(1)} %all-to-all-done.2.in_ref, f32[256,256]{1,0:T(8,128)S(1)} %get-tuple-element.25.sums_in, bf16[2,256,512]{2,1,0:T(8,128)(2,1)S(1)} %get-tuple-element.16.td_ref, bf16[2,256,512]{2,1,0:T(8,128)(2,1)S(1)} %get-tuple-element.17.gd_ref), custom_call_target="tpu_custom_call" | custom-call | tf_op jit(solution)/shard_map/sums/pallas_call | solution.py:223
  57.0 11.5 %all-to-all-start.3 = ((bf16[16,16,256]{2,1,0:T(8,128)(2,1)}), bf16[16,16,256]{2,1,0:T(8,128)(2,1)S(1)}, u32[]{:S(2)}, u32[]{:S(2)}) async-start(bf16[16,16,256]{2,1,0:T(8,128)(2,1)} %sums.1), calls=%async_computation.3 | async-start | bytes 262144 | tf_op jit(solution)/shard_map/all_to_all | solution.py:207
  68.5 0.5 finish.1
  69.0 0.7 copy.11
  69.7 0.7 copy.12
  70.4 4.8 %all-to-all-done.3.got_ref = bf16[16,16,256]{2,1,0:T(8,128)(2,1)S(1)} async-done(((bf16[16,16,256]{2,1,0:T(8,128)(2,1)}), bf16[16,16,256]{2,1,0:T(8,128)(2,1)S(1)}, u32[]{:S(2)}, u32[]{:S(2)}) %all-to-all-start.3) | async-done | bytes 131104 | tf_op jit(solution)/shard_map/all_to_all | solution.py:207
  75.2 0.6 total.1
Async XLA Ops:
  0.6 20.7 %copy-start = (bf16[256,512]{1,0:T(8,128)(2,1)S(1)}, bf16[256,512]{1,0:T(8,128)(2,1)}, u32[]{:S(2)}) copy-start(bf16[256,512]{1,0:T(8,128)(2,1)} %x_ref.3) | copy-start | bytes 786436
  2.1 19.3 %copy-start.3 = (s32[8,256]{1,0:T(8,128)S(1)}, s32[8,256]{1,0:T(8,128)}, u32[]{:S(2)}) copy-start(s32[8,256]{1,0:T(8,128)} %codes_ref.3) | copy-start | bytes 24580
  2.1 19.3 %copy-start.4 = (f32[8]{0:T(128)S(1)}, f32[8]{0:T(128)}, u32[]{:S(2)}) copy-start(f32[8]{0:T(128)} %rate_ref.3) | copy-start | bytes 100
  2.1 25.8 %all-to-all-start = ((bf16[16,32,128]{2,1,0:T(8,128)(2,1)}), bf16[16,32,128]{2,1,0:T(8,128)(2,1)S(1)}, u32[]{:S(2)}, u32[]{:S(2)}) async-start(bf16[16,32,128]{2,1,0:T(8,128)(2,1)} %broadcast_in_dim.2), calls=%async_computation | async-start | bytes 262144 | tf_op jit(solution)/shard_map/all_to_all | solution.py:207
  21.3 1.0 %copy-start.1 = (bf16[256,512]{1,0:T(8,128)(2,1)S(1)}, bf16[256,512]{1,0:T(8,128)(2,1)}, u32[]{:S(2)}) copy-start(bf16[256,512]{1,0:T(8,128)(2,1)} %dy_ref.3) | copy-start | bytes 786436
  43.6 8.2 %copy-start.2 = (bf16[256,512]{1,0:T(8,128)(2,1)S(1)}, bf16[256,512]{1,0:T(8,128)(2,1)}, u32[]{:S(2)}) copy-start(bf16[256,512]{1,0:T(8,128)(2,1)} %dy_ref.3) | copy-start | bytes 786436
  43.6 8.2 %copy-start.5 = (f32[8]{0:T(128)S(1)}, f32[8]{0:T(128)}, u32[]{:S(2)}) copy-start(f32[8]{0:T(128)} %gain_ref.1) | copy-start | bytes 100
  43.6 12.3 %all-to-all-start.2 = ((bf16[32,32,128]{2,1,0:T(8,128)(2,1)}), bf16[32,32,128]{2,1,0:T(8,128)(2,1)S(1)}, u32[]{:S(2)}, u32[]{:S(2)}) async-start(bf16[32,32,128]{2,1,0:T(8,128)(2,1)} %scan.1), calls=%async_computation.2 | async-start | bytes 524288 | tf_op jit(solution)/shard_map/all_to_all | solution.py:207
  57.0 18.1 %all-to-all-start.3 = ((bf16[16,16,256]{2,1,0:T(8,128)(2,1)}), bf16[16,16,256]{2,1,0:T(8,128)(2,1)S(1)}, u32[]{:S(2)}, u32[]{:S(2)}) async-start(bf16[16,16,256]{2,1,0:T(8,128)(2,1)} %sums.1), calls=%async_computation.3 | async-start | bytes 262144 | tf_op jit(solution)/shard_map/all_to_all | solution.py:207

commit v4 on v3

--- a/solution.py
+++ b/solution.py
@@ -78,7 +78,35 @@
     return b, c
 
 
-def prepare_kernel(x_ref, dy_ref, codes_ref, rate_ref, td_ref, gd_ref, grow_ref, dt_ref, e_ref):
+def causal_mask():
+    i = lax.broadcasted_iota(jnp.int32, (BLOCK, BLOCK), 0)
+    j = lax.broadcasted_iota(jnp.int32, (BLOCK, BLOCK), 1)
+    return i >= j
+
+
+def weight_maker(log_decay, cumul):
+    causal = causal_mask()
+    lower = jnp.where(causal, 1.0, 0.0).astype(BF)
+    cumul_t = sum(dg(lower, p, 1, 1) for p in pieces(log_decay, 3)[::-1])
+
+    def weights(h):
+        spread = cumul_t[:, h : h + 1] - cumul[h : h + 1, :]
+        return jnp.exp(jnp.where(causal, spread, -1e30))
+
+    return weights
+
+
+def pair_cut(pair):
+    return slice(pair * 2 * HEAD_DIM, (pair + 1) * 2 * HEAD_DIM)
+
+
+def first_half():
+    return lax.broadcasted_iota(jnp.int32, (BLOCK, 2 * HEAD_DIM), 1) < HEAD_DIM
+
+
+def prepare_kernel(
+    x_ref, dy_ref, codes_ref, rate_ref, td_ref, gd_ref, pr_ref, grow_ref, dt_ref, e_ref
+):
     delta, log_decay = decode(codes_ref[...], rate_ref)
     cumul = running_sum(log_decay)
     heads = delta.shape[0]
@@ -90,6 +118,18 @@
     gd_ref[0], gd_ref[1] = pieces(dy_ref[...].astype(F32) * expand(growth, heads), 2)
     grow_ref[...] = growth
     dt_ref[...] = stack(delta * tail, 3)
+    weights = weight_maker(log_decay, cumul)
+    first = first_half()
+    zero = jnp.zeros((BLOCK, 2 * HEAD_DIM), BF)
+    paired = jnp.zeros((BLOCK, BLOCK), F32)
+    for pair in range(heads // 2):
+        u, g = driven[:, pair_cut(pair)], dy_ref[:, pair_cut(pair)]
+        for side in range(2):
+            own = first if side == 0 else jnp.logical_not(first)
+            raw = dg(jnp.where(own, g, zero), u, 1, 1)
+            paired = paired + (weights(2 * pair + side) * raw).astype(BF).astype(F32)
+    pr_ref[0], pr_ref[1] = pieces(paired.T, 2)
+    pr_ref[2], pr_ref[3] = pieces(paired, 2)
     hi, mid, low = [p.astype(F32) for p in pieces(jnp.exp(total), 3)]
     row = lax.broadcasted_iota(jnp.int32, (8, STATE), 0)
     for h in range(heads):
@@ -119,86 +159,66 @@
     for k in slots:
         tile = got_ref[k, 32:40, :].astype(F32)
         decays[k] = tile[0:1] + tile[1:2] + tile[2:3]
-    run = jnp.zeros((16, STATE), F32)
-    for k in slots:
-        send_ref[k, 0:16, :] = run.astype(BF)
-        run = decays[k] * run + got_ref[k, 0:16, :].astype(F32)
-    run = jnp.zeros((16, STATE), F32)
-    for k in slots[::-1]:
-        send_ref[k, 16:32, :] = run.astype(BF)
-        run = decays[k] * run + got_ref[k, 16:32, :].astype(F32)
-
-
-def within_kernel(
-    bc_ref, x_ref, dy_ref, codes_ref, rate_ref, gain_ref, out_ref, grad_ref, sums_ref
+    ahead = behind = jnp.zeros((16, STATE), F32)
+    for k, m in zip(slots, slots[::-1]):
+        send_ref[k, 0:16, :] = ahead.astype(BF)
+        send_ref[m, 16:32, :] = behind.astype(BF)
+        ahead = decays[k] * ahead + got_ref[k, 0:16, :].astype(F32)
+        behind = decays[m] * behind + got_ref[m, 16:32, :].astype(F32)
+
+
+def sums_kernel(bc_ref, in_ref, pr_ref, td_ref, gd_ref, sums_ref):
+    b, c = both(bc_ref)
+    width = td_ref.shape[2]
+    groups, rows = sums_ref.shape[0], sums_ref.shape[1] // 2
+    order = turned(groups, HEAD_START)
+    for side, (parts, other) in enumerate(((td_ref, c), (gd_ref, b))):
+        carry = in_ref[:, 16 - 16 * side : 32 - 16 * side, :].reshape(width, STATE)
+        made = dg(pr_ref[2 * side], other, 1, 0) + dg(pr_ref[2 * side + 1], other, 1, 0)
+        made = (made + dg(parts[0], carry, 1, 0) + dg(parts[1], carry, 1, 0)).astype(BF)
+        for slot, g in enumerate(order):
+            sums_ref[slot, side * rows : (side + 1) * rows, :] = made[g * rows : (g + 1) * rows]
+
+
+def finish_kernel(
+    bc_ref, in_ref, grow_ref, dt_ref, x_ref, dy_ref, codes_ref, rate_ref, gain_ref, out_ref, grad_ref
 ):
     b, c = both(bc_ref)
     delta, log_decay = decode(codes_ref[...], rate_ref)
     cumul = running_sum(log_decay)
-    heads = cumul.shape[0]
+    heads = delta.shape[0]
+    width = heads * HEAD_DIM
     delta_x = expand(stack(delta, 2), heads)
     driven = (x_ref[...].astype(F32) * delta_x).astype(BF)
-    i = lax.broadcasted_iota(jnp.int32, (BLOCK, BLOCK), 0)
-    j = lax.broadcasted_iota(jnp.int32, (BLOCK, BLOCK), 1)
-    causal = i >= j
-    lower = jnp.where(causal, 1.0, 0.0).astype(BF)
-    cumul_t = sum(dg(lower, p, 1, 1) for p in pieces(log_decay, 3)[::-1])
+    state = in_ref[:, 0:16, :].reshape(width, STATE)
+    adjoint = in_ref[:, 16:32, :].reshape(width, STATE)
+    out_cross = expand(grow_ref[...], heads) * dg(c, state, 1, 1)
+    grad_cross = expand(dt_ref[...], heads) * dg(b, adjoint, 1, 1)
     scores = dg(c, b, 1, 1)
-    lane = lax.broadcasted_iota(jnp.int32, (BLOCK, 2 * HEAD_DIM), 1)
-    first = lane < HEAD_DIM
-    zero = jnp.zeros((BLOCK, 2 * HEAD_DIM), BF)
-    paired = jnp.zeros((BLOCK, BLOCK), F32)
+    weights = weight_maker(log_decay, cumul)
+    first = first_half()
     chan = lax.broadcasted_iota(jnp.int32, (1, 2 * HEAD_DIM), 1)
     for pair in range(heads // 2):
-        cut = slice(pair * 2 * HEAD_DIM, (pair + 1) * 2 * HEAD_DIM)
+        cut = pair_cut(pair)
         u, g = driven[:, cut], dy_ref[:, cut]
         made = []
         for side in range(2):
-            h = 2 * pair + side
-            spread = cumul_t[:, h : h + 1] - cumul[h : h + 1, :]
-            weights = jnp.exp(jnp.where(causal, spread, -1e30))
-            mixed = (weights * scores).astype(BF)
-            own = first if side == 0 else jnp.logical_not(first)
-            raw = dg(jnp.where(own, g, zero), u, 1, 1)
-            paired = paired + (weights * raw).astype(BF).astype(F32)
+            mixed = (weights(2 * pair + side) * scores).astype(BF)
             made.append((dg(mixed, u, 1, 0), dg(mixed, g, 0, 0)))
         gain = jnp.where(chan < HEAD_DIM, gain_ref[2 * pair], gain_ref[2 * pair + 1])
-        out_ref[:, cut] = jnp.where(first, made[0][0], made[1][0]) + gain * x_ref[:, cut].astype(F32)
-        grad_ref[:, cut] = (
-            jnp.where(first, made[0][1], made[1][1]) * delta_x[:, cut] + gain * g.astype(F32)
-        )
-    sums_ref[:, 0:STATE] = split_dot(paired, c, 0, 0)
-    sums_ref[:, STATE:] = split_dot(paired, b, 1, 0)
-
-
-def sums_kernel(in_ref, sums_in, td_ref, gd_ref, sums_ref):
-    width = td_ref.shape[2]
-    state = in_ref[:, 0:16, :].reshape(width, STATE)
-    adjoint = in_ref[:, 16:32, :].reshape(width, STATE)
-    groups, rows = sums_ref.shape[:2]
-    b_sum = sums_in[:, 0:STATE] + dg(td_ref[0], adjoint, 1, 0) + dg(td_ref[1], adjoint, 1, 0)
-    c_sum = sums_in[:, STATE:] + dg(gd_ref[0], state, 1, 0) + dg(gd_ref[1], state, 1, 0)
-    for slot, g in enumerate(turned(groups, HEAD_START)):
-        sums_ref[slot, :, 0:STATE] = b_sum[g * rows : (g + 1) * rows].astype(BF)
-        sums_ref[slot, :, STATE:] = c_sum[g * rows : (g + 1) * rows].astype(BF)
-
-
-def finish_kernel(bc_ref, in_ref, out_in, grad_in, grow_ref, dt_ref, out_ref, grad_ref):
-    b, c = both(bc_ref)
-    width = out_in.shape[1]
-    heads = width // HEAD_DIM
-    state = in_ref[:, 0:16, :].reshape(width, STATE)
-    adjoint = in_ref[:, 16:32, :].reshape(width, STATE)
-    out_ref[...] = (out_in[...] + expand(grow_ref[...], heads) * dg(c, state, 1, 1)).astype(BF)
-    grad_ref[...] = (grad_in[...] + expand(dt_ref[...], heads) * dg(b, adjoint, 1, 1)).astype(BF)
+        out = jnp.where(first, made[0][0], made[1][0]) + out_cross[:, cut]
+        grad = jnp.where(first, made[0][1], made[1][1]) * delta_x[:, cut] + grad_cross[:, cut]
+        out_ref[:, cut] = (out + gain * x_ref[:, cut].astype(F32)).astype(BF)
+        grad_ref[:, cut] = (grad + gain * g.astype(F32)).astype(BF)
 
 
 def total_kernel(got_ref, b_ref, c_ref):
     acc = got_ref[0].astype(F32)
     for k in range(1, got_ref.shape[0]):
         acc = acc + got_ref[k].astype(F32)
-    b_ref[...] = acc[:, 0:STATE]
-    c_ref[...] = acc[:, STATE:]
+    rows = b_ref.shape[0]
+    b_ref[...] = acc[0:rows]
+    c_ref[...] = acc[rows:]
 
 
 def exchange(x, axis):
@@ -238,12 +258,13 @@
     wide = x_in.shape
     mine = jnp.concatenate([b_in, c_in], axis=0)
     bc = exchange(jnp.broadcast_to(mine[None], (groups, 2 * rows, STATE)), "head")
-    td, gd, grow, dt, e = kernel(
+    td, gd, paired, grow, dt, e = kernel(
         prepare_kernel,
         "prepare",
         [
             ((2,) + wide, BF),
             ((2,) + wide, BF),
+            ((4, tokens, tokens), BF),
             ((3 * heads, tokens), BF),
             ((3 * heads, tokens), BF),
             ((heads, 8, STATE), BF),
@@ -257,23 +278,10 @@
     )
     send = kernel(summary_kernel, "summary", [((seqs, 40, STATE), BF)], bc, td, gd, e)
     got = exchange(send, "seq")
-    out_part, grad_part, sums_part = kernel(
-        within_kernel,
-        "within",
-        [(wide, F32), (wide, F32), ((tokens, 2 * STATE), F32)],
-        bc,
-        x_in,
-        out_grad,
-        decay_codes,
-        decay_rate,
-        skip_gain,
-        scalars=(4, 5),
-        far=(1, 2, 3),
-    )
     back = kernel(scan_kernel, "scan", [((seqs, 32, STATE), BF)], got)
     carried = exchange(back, "seq")
     sums = kernel(
-        sums_kernel, "sums", [((groups, rows, 2 * STATE), BF)], carried, sums_part, td, gd
+        sums_kernel, "sums", [((groups, 2 * rows, STATE), BF)], bc, carried, paired, td, gd
     )
     totals = exchange(sums, "head")
     ssm_out, input_grad = kernel(
@@ -282,10 +290,15 @@
         [(wide, BF), (wide, BF)],
         bc,
         carried,
-        out_part,
-        grad_part,
         grow,
         dt,
+        x_in,
+        out_grad,
+        decay_codes,
+        decay_rate,
+        skip_gain,
+        scalars=(7, 8),
+        far=(4, 5, 6),
     )
     grad_b, grad_c = kernel(
         total_kernel, "total", [((rows, STATE), F32)] * 2, totals, kept=False

time: 76.3 us -> 75.4 us (0.988)
  blocking collectives: 14.5 us -> 26.5 us
  starting transfers between devices: 38.9 us -> 30.8 us
  waiting for transfers between devices: 10.8 us -> 5.63 us
    all_to_all x1 -> x2, blocking collectives: 14.5 us -> 26.5 us  [exchange(): return lax.all_to_all(x, axis, 0, 0, tiled=True, axis_index_groups=[order])]
    all_to_all x3 -> x2, starting transfers between devices: 38.9 us -> 30.8 us  [exchange(): return lax.all_to_all(x, axis, 0, 0, tiled=True, axis_index_groups=[order])]
    all_to_all x3 -> x2, waiting for transfers between devices: 10.8 us -> 5.63 us  [exchange(): return lax.all_to_all(x, axis, 0, 0, tiled=True, axis_index_groups=[order])]
    pallas_call x7 -> x6, Pallas kernels: 7.11 us -> 6.9 us  [kernel(): pl.pallas_call(body, out_shape=shapes, in_specs=specs, out_specs=tuple((p...]
  transfers between devices with their start and end apart: 3 -> 2, of which waited for: 3 -> 2; matrix products, arithmetic and copies ran while one was open for 2% -> 2% of each run, Pallas kernels for 5% -> 6%
where the time goes in v4:
time: 75.4 us; the launch traced here: 75 us
  starting transfers between devices  30.8 us (41%)
  blocking collectives  26.5 us (35%)
  Pallas kernels  6.9 us (9%)
  waiting for transfers between devices  5.63 us (7%)
  local copies, waits for them, and re-layouts  3.68 us (5%)
    all_to_all x2, starting transfers between devices, exchange(): return lax.all_to_all(x, axis, 0, 0, tiled=True, axis_index_groups=[order])  30.8 us
    all_to_all x2, blocking collectives, exchange(): return lax.all_to_all(x, axis, 0, 0, tiled=True, axis_index_groups=[order])  26.5 us
    pallas_call x6, Pallas kernels, kernel(): pl.pallas_call(body, out_shape=shapes, in_specs=specs, out_specs=tuple((p...  6.9 us
    all_to_all x2, waiting for transfers between devices, exchange(): return lax.all_to_all(x, axis, 0, 0, tiled=True, axis_index_groups=[order])  5.63 us
    unnamed x14, local copies, waits for them, and re-layouts  3.01 us
  transfers between devices with their start and end apart: 2, of which 2 were waited for; matrix products, arithmetic and copies ran while one was open for 2% of the time, Pallas kernels for 6%

profile of v4, /device:TPU:1, one launch (start us, length us, event | category | flops | bytes accessed | tf_op | source)
XLA Modules:
  0.0 75.0 jit_solution(3925239172482234819)
XLA Ops:
  0.6 0.0 copy-start
  0.6 0.7 pad_maximum_fusion
  1.4 0.7 broadcast_in_dim.2
  2.1 0.0 copy-start.3
  2.1 0.0 copy-start.4
  2.1 19.2 %all-to-all-start = ((bf16[16,32,128]{2,1,0:T(8,128)(2,1)}), bf16[16,32,128]{2,1,0:T(8,128)(2,1)S(1)}, u32[]{:S(2)}, u32[]{:S(2)}) async-start(bf16[16,32,128]{2,1,0:T(8,128)(2,1)} %broadcast_in_dim.2), calls=%async_computation | async-start | bytes 262144 | tf_op jit(solution)/shard_map/all_to_all | solution.py:227
  21.3 0.0 copy-done
  21.3 0.0 copy-done.3
  21.3 0.0 copy-done.4
  21.3 0.0 copy-start.1
  21.3 0.9 %copy-done.1 = bf16[256,512]{1,0:T(8,128)(2,1)S(1)} copy-done((bf16[256,512]{1,0:T(8,128)(2,1)S(1)}, bf16[256,512]{1,0:T(8,128)(2,1)}, u32[]{:S(2)}) %copy-start.1) | copy-done | bytes 262168
  22.3 2.0 %prepare.1 = (bf16[2,256,512]{2,1,0:T(8,128)(2,1)S(1)}, bf16[2,256,512]{2,1,0:T(8,128)(2,1)S(1)}, bf16[4,256,256]{2,1,0:T(8,128)(2,1)S(1)}, bf16[24,256]{1,0:T(8...) custom-call(bf16[256,512]{1,0:T(8,128)(2,1)S(1)} %copy-done, bf16[256,512]{1,0:T(8,128)(2,1)S(1)} %copy-done.1, ...), custom_call_target="tpu_custom_call" | custom-call | tf_op jit(solution)/shard_map/prepare/pallas_call | solution.py:243
  24.3 3.5 %all-to-all-done.bc_ref = bf16[16,32,128]{2,1,0:T(8,128)(2,1)S(1)} async-done(((bf16[16,32,128]{2,1,0:T(8,128)(2,1)}), bf16[16,32,128]{2,1,0:T(8,128)(2,1)S(1)}, u32[]{:S(2)}, u32[]{:S(2)}) %all-to-all-start) | async-done | bytes 131104 | tf_op jit(solution)/shard_map/all_to_all | solution.py:227
  27.8 0.5 summary.1
  28.3 14.5 %all_to_all.20.got_ref = bf16[32,40,128]{2,1,0:T(8,128)(2,1)S(1)} all-to-all(bf16[32,40,128]{2,1,0:T(8,128)(2,1)S(1)} %summary.1), channel_id=1, replica_groups={{320,336,352,368,384,400,416,432,448,464,480,496,0,16,32,48,64,80,96,11..., dimensions={0} | all-to-all | bytes 655360 | tf_op jit(solution)/shard_map/all_to_all | solution.py:227
  42.8 0.1 scan.1
  42.9 12.0 %all_to_all.21.in_ref = bf16[32,32,128]{2,1,0:T(8,128)(2,1)S(1)} all-to-all(bf16[32,32,128]{2,1,0:T(8,128)(2,1)S(1)} %scan.1), channel_id=1, replica_groups={{320,336,352,368,384,400,416,432,448,464,480,496,0,16,32,48,64,80,96,11..., dimensions={0} | all-to-all | bytes 524288 | tf_op jit(solution)/shard_map/all_to_all | solution.py:227
  54.9 1.2 %sums.1 = bf16[16,32,128]{2,1,0:T(8,128)(2,1)} custom-call(bf16[16,32,128]{2,1,0:T(8,128)(2,1)S(1)} %all-to-all-done.bc_ref, bf16[32,32,128]{2,1,0:T(8,128)(2,1)S(1)} %all_to_all.21.in_ref, bf16[4,256,256]{2,1,0:T(8,128)(2,1)S(1)} %get-tuple-element.21.pr_ref, bf16[2,256,512]{2,1,0:T(8,128)(2,1)S(1)} %get-tuple-element.14.td_ref, ...), custom_call_target="tpu_custom_call" | custom-call | tf_op jit(solution)/shard_map/sums/pallas_call | solution.py:243
  56.1 0.0 copy-start.2
  56.1 11.6 %all-to-all-start.3 = ((bf16[16,32,128]{2,1,0:T(8,128)(2,1)}), bf16[16,32,128]{2,1,0:T(8,128)(2,1)S(1)}, u32[]{:S(2)}, u32[]{:S(2)}) async-start(bf16[16,32,128]{2,1,0:T(8,128)(2,1)} %sums.1), calls=%async_computation.3 | async-start | bytes 262144 | tf_op jit(solution)/shard_map/all_to_all | solution.py:227
  67.7 0.0 copy-start.5
  67.7 0.0 copy-done.2
  67.7 0.6 copy-done.5
  68.3 2.5 %finish.1 = (bf16[256,512]{1,0:T(8,128)(2,1)S(1)}, bf16[256,512]{1,0:T(8,128)(2,1)S(1)}) custom-call(bf16[16,32,128]{2,1,0:T(8,128)(2,1)S(1)} %all-to-all-done.bc_ref, bf16[32,32,128]{2,1,0:T(8,128)(2,1)S(1)} %all_to_all.21.in_ref, bf16[24,256]{1,0:T(8,128)(2,1)S(1)} %get-tuple-element.17.grow_ref, bf16[24,256]{1,0:T(8,128)(2,1)S(1)} %get-tuple-element.18.dt_ref, ...), custom_call_target="tpu_custom_call" | custom-call | tf_op jit(solution)/shard_map/finish/pallas_call | solution.py:243
  70.8 0.7 copy.11
  71.6 0.7 copy.12
  72.3 2.1 %all-to-all-done.3.got_ref = bf16[16,32,128]{2,1,0:T(8,128)(2,1)S(1)} async-done(((bf16[16,32,128]{2,1,0:T(8,128)(2,1)}), bf16[16,32,128]{2,1,0:T(8,128)(2,1)S(1)}, u32[]{:S(2)}, u32[]{:S(2)}) %all-to-all-start.3) | async-done | bytes 131104 | tf_op jit(solution)/shard_map/all_to_all | solution.py:227
  74.4 0.6 total.1
Async XLA Ops:
  0.6 20.7 %copy-start = (bf16[256,512]{1,0:T(8,128)(2,1)S(1)}, bf16[256,512]{1,0:T(8,128)(2,1)}, u32[]{:S(2)}) copy-start(bf16[256,512]{1,0:T(8,128)(2,1)} %x_ref.3) | copy-start | bytes 786436
  2.1 19.3 %copy-start.3 = (s32[8,256]{1,0:T(8,128)S(1)}, s32[8,256]{1,0:T(8,128)}, u32[]{:S(2)}) copy-start(s32[8,256]{1,0:T(8,128)} %codes_ref.3) | copy-start | bytes 24580
  2.1 19.3 %copy-start.4 = (f32[8]{0:T(128)S(1)}, f32[8]{0:T(128)}, u32[]{:S(2)}) copy-start(f32[8]{0:T(128)} %rate_ref.3) | copy-start | bytes 100
  2.1 25.8 %all-to-all-start = ((bf16[16,32,128]{2,1,0:T(8,128)(2,1)}), bf16[16,32,128]{2,1,0:T(8,128)(2,1)S(1)}, u32[]{:S(2)}, u32[]{:S(2)}) async-start(bf16[16,32,128]{2,1,0:T(8,128)(2,1)} %broadcast_in_dim.2), calls=%async_computation | async-start | bytes 262144 | tf_op jit(solution)/shard_map/all_to_all | solution.py:227
  21.3 1.0 %copy-start.1 = (bf16[256,512]{1,0:T(8,128)(2,1)S(1)}, bf16[256,512]{1,0:T(8,128)(2,1)}, u32[]{:S(2)}) copy-start(bf16[256,512]{1,0:T(8,128)(2,1)} %dy_ref.3) | copy-start | bytes 786436
  56.1 11.6 %copy-start.2 = (bf16[256,512]{1,0:T(8,128)(2,1)S(1)}, bf16[256,512]{1,0:T(8,128)(2,1)}, u32[]{:S(2)}) copy-start(bf16[256,512]{1,0:T(8,128)(2,1)} %dy_ref.3) | copy-start | bytes 786436
  56.1 18.3 %all-to-all-start.3 = ((bf16[16,32,128]{2,1,0:T(8,128)(2,1)}), bf16[16,32,128]{2,1,0:T(8,128)(2,1)S(1)}, u32[]{:S(2)}, u32[]{:S(2)}) async-start(bf16[16,32,128]{2,1,0:T(8,128)(2,1)} %sums.1), calls=%async_computation.3 | async-start | bytes 262144 | tf_op jit(solution)/shard_map/all_to_all | solution.py:227
  67.7 0.7 copy-start.5

commit v5 on v4

--- a/solution.py
+++ b/solution.py
@@ -256,8 +256,8 @@
     rows = b_in.shape[0]
     heads, tokens = decay_codes.shape
     wide = x_in.shape
-    mine = jnp.concatenate([b_in, c_in], axis=0)
-    bc = exchange(jnp.broadcast_to(mine[None], (groups, 2 * rows, STATE)), "head")
+    spread = [jnp.broadcast_to(v[None], (groups, rows, STATE)) for v in (b_in, c_in)]
+    bc = exchange(jnp.concatenate(spread, axis=1), "head")
     td, gd, paired, grow, dt, e = kernel(
         prepare_kernel,
         "prepare",

time: 75.4 us -> 75.2 us (level)
  waiting for transfers between devices: 5.63 us -> 6.57 us
  local copies, waits for them, and re-layouts: 3.68 us -> 2.8 us
    all_to_all x2, waiting for transfers between devices: 5.63 us -> 6.57 us  [exchange(): return lax.all_to_all(x, axis, 0, 0, tiled=True, axis_index_groups=[order])]
    unnamed x14, local copies, waits for them, and re-layouts: 3.01 us -> 2.09 us
where the time goes in v5:
time: 75.2 us; the launch traced here: 74.7 us
  starting transfers between devices  30.6 us (41%)
  blocking collectives  26.5 us (35%)
  Pallas kernels  6.91 us (9%)
  waiting for transfers between devices  6.57 us (9%)
  local copies, waits for them, and re-layouts  2.8 us (4%)
    all_to_all x2, starting transfers between devices, exchange(): return lax.all_to_all(x, axis, 0, 0, tiled=True, axis_index_groups=[order])  30.6 us
    all_to_all x2, blocking collectives, exchange(): return lax.all_to_all(x, axis, 0, 0, tiled=True, axis_index_groups=[order])  26.5 us
    pallas_call x6, Pallas kernels, kernel(): pl.pallas_call(body, out_shape=shapes, in_specs=specs, out_specs=tuple((p...  6.91 us
    all_to_all x2, waiting for transfers between devices, exchange(): return lax.all_to_all(x, axis, 0, 0, tiled=True, axis_index_groups=[order])  6.57 us
    unnamed x14, local copies, waits for them, and re-layouts  2.09 us
  transfers between devices with their start and end apart: 2, of which 2 were waited for; matrix products, arithmetic and copies ran while one was open for 2% of the time, Pallas kernels for 6%

profile of v5, /device:TPU:1, one launch (start us, length us, event | category | flops | bytes accessed | tf_op | source)
XLA Modules:
  0.0 74.7 jit_solution(9208400873084597074)
XLA Ops:
  0.6 0.0 copy-start.5
  0.6 0.7 broadcast_in_dim.4
  1.3 0.0 copy-done.5
  1.4 0.0 copy-start.2
  1.4 0.0 copy-start.3
  1.4 0.0 copy-start
  1.4 0.0 copy-start.1
  1.4 0.7 pad_maximum_fusion
  2.1 19.1 %all-to-all-start = ((bf16[16,32,128]{2,1,0:T(8,128)(2,1)}), bf16[16,32,128]{2,1,0:T(8,128)(2,1)S(1)}, u32[]{:S(2)}, u32[]{:S(2)}) async-start(bf16[16,32,128]{2,1,0:T(8,128)(2,1)} %pad_maximum_fusion), calls=%async_computation | async-start | bytes 262144 | tf_op jit(solution)/shard_map/all_to_all | solution.py:227
  21.2 0.0 copy-done.2
  21.2 0.0 copy-done.3
  21.2 0.0 copy-done
  21.2 0.0 copy-done.1
  21.2 2.0 %prepare.1 = (bf16[2,256,512]{2,1,0:T(8,128)(2,1)S(1)}, bf16[2,256,512]{2,1,0:T(8,128)(2,1)S(1)}, bf16[4,256,256]{2,1,0:T(8,128)(2,1)S(1)}, bf16[24,256]{1,0:T(8...) custom-call(bf16[256,512]{1,0:T(8,128)(2,1)S(1)} %copy-done, bf16[256,512]{1,0:T(8,128)(2,1)S(1)} %copy-done.1, ...), custom_call_target="tpu_custom_call" | custom-call | tf_op jit(solution)/shard_map/prepare/pallas_call | solution.py:243
  23.2 4.5 %all-to-all-done.bc_ref = bf16[16,32,128]{2,1,0:T(8,128)(2,1)S(1)} async-done(((bf16[16,32,128]{2,1,0:T(8,128)(2,1)}), bf16[16,32,128]{2,1,0:T(8,128)(2,1)S(1)}, u32[]{:S(2)}, u32[]{:S(2)}) %all-to-all-start) | async-done | bytes 131104 | tf_op jit(solution)/shard_map/all_to_all | solution.py:227
  27.7 0.5 summary.1
  28.2 14.5 %all_to_all.20.got_ref = bf16[32,40,128]{2,1,0:T(8,128)(2,1)S(1)} all-to-all(bf16[32,40,128]{2,1,0:T(8,128)(2,1)S(1)} %summary.1), channel_id=1, replica_groups={{320,336,352,368,384,400,416,432,448,464,480,496,0,16,32,48,64,80,96,11..., dimensions={0} | all-to-all | bytes 655360 | tf_op jit(solution)/shard_map/all_to_all | solution.py:227
  42.7 0.1 scan.1
  42.8 12.0 %all_to_all.21.in_ref = bf16[32,32,128]{2,1,0:T(8,128)(2,1)S(1)} all-to-all(bf16[32,32,128]{2,1,0:T(8,128)(2,1)S(1)} %scan.1), channel_id=1, replica_groups={{320,336,352,368,384,400,416,432,448,464,480,496,0,16,32,48,64,80,96,11..., dimensions={0} | all-to-all | bytes 524288 | tf_op jit(solution)/shard_map/all_to_all | solution.py:227
  54.8 1.2 %sums.1 = bf16[16,32,128]{2,1,0:T(8,128)(2,1)} custom-call(bf16[16,32,128]{2,1,0:T(8,128)(2,1)S(1)} %all-to-all-done.bc_ref, bf16[32,32,128]{2,1,0:T(8,128)(2,1)S(1)} %all_to_all.21.in_ref, bf16[4,256,256]{2,1,0:T(8,128)(2,1)S(1)} %get-tuple-element.21.pr_ref, bf16[2,256,512]{2,1,0:T(8,128)(2,1)S(1)} %get-tuple-element.14.td_ref, ...), custom_call_target="tpu_custom_call" | custom-call | tf_op jit(solution)/shard_map/sums/pallas_call | solution.py:243
  56.0 11.5 %all-to-all-start.3 = ((bf16[16,32,128]{2,1,0:T(8,128)(2,1)}), bf16[16,32,128]{2,1,0:T(8,128)(2,1)S(1)}, u32[]{:S(2)}, u32[]{:S(2)}) async-start(bf16[16,32,128]{2,1,0:T(8,128)(2,1)} %sums.1), calls=%async_computation.3 | async-start | bytes 262144 | tf_op jit(solution)/shard_map/all_to_all | solution.py:227
  67.4 0.0 copy-start.4
  67.4 0.6 copy-done.4
  68.1 2.5 %finish.1 = (bf16[256,512]{1,0:T(8,128)(2,1)S(1)}, bf16[256,512]{1,0:T(8,128)(2,1)S(1)}) custom-call(bf16[16,32,128]{2,1,0:T(8,128)(2,1)S(1)} %all-to-all-done.bc_ref, bf16[32,32,128]{2,1,0:T(8,128)(2,1)S(1)} %all_to_all.21.in_ref, bf16[24,256]{1,0:T(8,128)(2,1)S(1)} %get-tuple-element.17.grow_ref, bf16[24,256]{1,0:T(8,128)(2,1)S(1)} %get-tuple-element.18.dt_ref, ...), custom_call_target="tpu_custom_call" | custom-call | tf_op jit(solution)/shard_map/finish/pallas_call | solution.py:243
  70.6 0.7 copy.11
  71.3 0.7 copy.12
  72.0 2.1 %all-to-all-done.3.got_ref = bf16[16,32,128]{2,1,0:T(8,128)(2,1)S(1)} async-done(((bf16[16,32,128]{2,1,0:T(8,128)(2,1)}), bf16[16,32,128]{2,1,0:T(8,128)(2,1)S(1)}, u32[]{:S(2)}, u32[]{:S(2)}) %all-to-all-start.3) | async-done | bytes 131104 | tf_op jit(solution)/shard_map/all_to_all | solution.py:227
  74.1 0.6 total.1
  (1 shorter events, 0.0 us)
Async XLA Ops:
  0.6 0.7 copy-start.5
  1.4 19.8 %copy-start.2 = (s32[8,256]{1,0:T(8,128)S(1)}, s32[8,256]{1,0:T(8,128)}, u32[]{:S(2)}) copy-start(s32[8,256]{1,0:T(8,128)} %codes_ref.3) | copy-start | bytes 24580
  1.4 19.8 %copy-start.3 = (f32[8]{0:T(128)S(1)}, f32[8]{0:T(128)}, u32[]{:S(2)}) copy-start(f32[8]{0:T(128)} %rate_ref.3) | copy-start | bytes 100
  1.4 19.8 %copy-start = (bf16[256,512]{1,0:T(8,128)(2,1)S(1)}, bf16[256,512]{1,0:T(8,128)(2,1)}, u32[]{:S(2)}) copy-start(bf16[256,512]{1,0:T(8,128)(2,1)} %x_ref.3) | copy-start | bytes 786436
  1.4 19.8 %copy-start.1 = (bf16[256,512]{1,0:T(8,128)(2,1)S(1)}, bf16[256,512]{1,0:T(8,128)(2,1)}, u32[]{:S(2)}) copy-start(bf16[256,512]{1,0:T(8,128)(2,1)} %dy_ref.3) | copy-start | bytes 786436
  2.1 25.6 %all-to-all-start = ((bf16[16,32,128]{2,1,0:T(8,128)(2,1)}), bf16[16,32,128]{2,1,0:T(8,128)(2,1)S(1)}, u32[]{:S(2)}, u32[]{:S(2)}) async-start(bf16[16,32,128]{2,1,0:T(8,128)(2,1)} %pad_maximum_fusion), calls=%async_computation | async-start | bytes 262144 | tf_op jit(solution)/shard_map/all_to_all | solution.py:227
  56.0 18.1 %all-to-all-start.3 = ((bf16[16,32,128]{2,1,0:T(8,128)(2,1)}), bf16[16,32,128]{2,1,0:T(8,128)(2,1)S(1)}, u32[]{:S(2)}, u32[]{:S(2)}) async-start(bf16[16,32,128]{2,1,0:T(8,128)(2,1)} %sums.1), calls=%async_computation.3 | async-start | bytes 262144 | tf_op jit(solution)/shard_map/all_to_all | solution.py:227
  67.4 0.7 copy-start.4

commit v6 on v5

--- a/solution.py
+++ b/solution.py
@@ -105,7 +105,7 @@
 
 
 def prepare_kernel(
-    x_ref, dy_ref, codes_ref, rate_ref, td_ref, gd_ref, pr_ref, grow_ref, dt_ref, e_ref
+    x_ref, dy_ref, codes_ref, rate_ref, td_ref, gd_ref, tt_ref, gt_ref, pr_ref, grow_ref, dt_ref, e_ref
 ):
     delta, log_decay = decode(codes_ref[...], rate_ref)
     cumul = running_sum(log_decay)
@@ -114,8 +114,14 @@
     growth = stack(jnp.exp(cumul), 3)
     tail = jnp.exp(total - cumul)
     driven = (x_ref[...].astype(F32) * expand(stack(delta, 2), heads)).astype(BF)
-    td_ref[0], td_ref[1] = pieces(driven.astype(F32) * expand(stack(tail, 3), heads), 2)
-    gd_ref[0], gd_ref[1] = pieces(dy_ref[...].astype(F32) * expand(growth, heads), 2)
+    for wide_ref, turned_ref, value in (
+        (td_ref, tt_ref, driven.astype(F32) * expand(stack(tail, 3), heads)),
+        (gd_ref, gt_ref, dy_ref[...].astype(F32) * expand(growth, heads)),
+    ):
+        for k, part in enumerate(pieces(value, 2)):
+            width = part.shape[1]
+            wide_ref[:, k * width : (k + 1) * width] = part
+            turned_ref[:, k * BLOCK : (k + 1) * BLOCK] = part.T
     grow_ref[...] = growth
     dt_ref[...] = stack(delta * tail, 3)
     weights = weight_maker(log_decay, cumul)
@@ -128,8 +134,9 @@
             own = first if side == 0 else jnp.logical_not(first)
             raw = dg(jnp.where(own, g, zero), u, 1, 1)
             paired = paired + (weights(2 * pair + side) * raw).astype(BF).astype(F32)
-    pr_ref[0], pr_ref[1] = pieces(paired.T, 2)
-    pr_ref[2], pr_ref[3] = pieces(paired, 2)
+    for side, value in enumerate((paired.T, paired)):
+        for k, part in enumerate(pieces(value, 2)):
+            pr_ref[side, :, k * BLOCK : (k + 1) * BLOCK] = part
     hi, mid, low = [p.astype(F32) for p in pieces(jnp.exp(total), 3)]
     row = lax.broadcasted_iota(jnp.int32, (8, STATE), 0)
     for h in range(heads):
@@ -138,11 +145,15 @@
         ).astype(BF)
 
 
-def summary_kernel(bc_ref, td_ref, gd_ref, e_ref, send_ref):
+def twice(v):
+    return jnp.concatenate([v, v], axis=0)
+
+
+def summary_kernel(bc_ref, tt_ref, gt_ref, e_ref, send_ref):
     b, c = both(bc_ref)
     parts, heads = send_ref.shape[0], e_ref.shape[0]
-    state = dg(td_ref[0], b, 0, 0) + dg(td_ref[1], b, 0, 0)
-    adjoint = dg(gd_ref[0], c, 0, 0) + dg(gd_ref[1], c, 0, 0)
+    state = dg(tt_ref[...], twice(b), 1, 0)
+    adjoint = dg(gt_ref[...], twice(c), 1, 0)
     send_ref[:, 0:16, :] = state.astype(BF).reshape(parts, 16, STATE)
     send_ref[:, 16:32, :] = adjoint.astype(BF).reshape(parts, 16, STATE)
     per = parts // heads
@@ -169,13 +180,13 @@
 
 def sums_kernel(bc_ref, in_ref, pr_ref, td_ref, gd_ref, sums_ref):
     b, c = both(bc_ref)
-    width = td_ref.shape[2]
+    width = td_ref.shape[1] // 2
     groups, rows = sums_ref.shape[0], sums_ref.shape[1] // 2
     order = turned(groups, HEAD_START)
     for side, (parts, other) in enumerate(((td_ref, c), (gd_ref, b))):
         carry = in_ref[:, 16 - 16 * side : 32 - 16 * side, :].reshape(width, STATE)
-        made = dg(pr_ref[2 * side], other, 1, 0) + dg(pr_ref[2 * side + 1], other, 1, 0)
-        made = (made + dg(parts[0], carry, 1, 0) + dg(parts[1], carry, 1, 0)).astype(BF)
+        made = dg(pr_ref[side], twice(other), 1, 0) + dg(parts[...], twice(carry), 1, 0)
+        made = made.astype(BF)
         for slot, g in enumerate(order):
             sums_ref[slot, side * rows : (side + 1) * rows, :] = made[g * rows : (g + 1) * rows]
 
@@ -258,13 +269,15 @@
     wide = x_in.shape
     spread = [jnp.broadcast_to(v[None], (groups, rows, STATE)) for v in (b_in, c_in)]
     bc = exchange(jnp.concatenate(spread, axis=1), "head")
-    td, gd, paired, grow, dt, e = kernel(
+    td, gd, tt, gt, paired, grow, dt, e = kernel(
         prepare_kernel,
         "prepare",
         [
-            ((2,) + wide, BF),
-            ((2,) + wide, BF),
-            ((4, tokens, tokens), BF),
+            ((tokens, 2 * wide[1]), BF),
+            ((tokens, 2 * wide[1]), BF),
+            ((wide[1], 2 * tokens), BF),
+            ((wide[1], 2 * tokens), BF),
+            ((2, tokens, 2 * tokens), BF),
             ((3 * heads, tokens), BF),
             ((3 * heads, tokens), BF),
             ((heads, 8, STATE), BF),
@@ -276,7 +289,7 @@
         scalars=(3,),
         far=(0, 1, 2),
     )
-    send = kernel(summary_kernel, "summary", [((seqs, 40, STATE), BF)], bc, td, gd, e)
+    send = kernel(summary_kernel, "summary", [((seqs, 40, STATE), BF)], bc, tt, gt, e)
     got = exchange(send, "seq")
     back = kernel(scan_kernel, "scan", [((seqs, 32, STATE), BF)], got)
     carried = exchange(back, "seq")

time: 75.2 us -> 75.3 us (level)
    unnamed x14 -> x22, local copies, waits for them, and re-layouts: 2.09 us -> 2.08 us
where the time goes in v6:
time: 75.3 us; the launch traced here: 74.8 us
  starting transfers between devices  30.7 us (41%)
  blocking collectives  26.5 us (35%)
  Pallas kernels  6.93 us (9%)
  waiting for transfers between devices  6.48 us (9%)
  local copies, waits for them, and re-layouts  2.8 us (4%)
  between operations  0.79 us (1%)
    all_to_all x2, starting transfers between devices, exchange(): return lax.all_to_all(x, axis, 0, 0, tiled=True, axis_index_groups=[order])  30.7 us
    all_to_all x2, blocking collectives, exchange(): return lax.all_to_all(x, axis, 0, 0, tiled=True, axis_index_groups=[order])  26.5 us
    pallas_call x6, Pallas kernels, kernel(): pl.pallas_call(body, out_shape=shapes, in_specs=specs, out_specs=tuple((p...  6.93 us
    all_to_all x2, waiting for transfers between devices, exchange(): return lax.all_to_all(x, axis, 0, 0, tiled=True, axis_index_groups=[order])  6.48 us
    unnamed x22, local copies, waits for them, and re-layouts  2.08 us
  transfers between devices with their start and end apart: 2, of which 2 were waited for; matrix products, arithmetic and copies ran while one was open for 2% of the time, Pallas kernels for 6%

profile of v6, /device:TPU:1, one launch (start us, length us, event | category | flops | bytes accessed | tf_op | source)
XLA Modules:
  0.0 74.8 jit_solution(13744663545404006073)
XLA Ops:
  0.6 0.0 copy-start.9
  0.6 0.7 broadcast_in_dim.4
  1.3 0.0 copy-done.9
  1.4 0.0 copy-start.2
  1.4 0.0 copy-start.7
  1.4 0.0 copy-start
  1.4 0.0 copy-start.1
  1.4 0.7 pad_maximum_fusion
  2.1 19.1 %all-to-all-start = ((bf16[16,32,128]{2,1,0:T(8,128)(2,1)}), bf16[16,32,128]{2,1,0:T(8,128)(2,1)S(1)}, u32[]{:S(2)}, u32[]{:S(2)}) async-start(bf16[16,32,128]{2,1,0:T(8,128)(2,1)} %pad_maximum_fusion), calls=%async_computation | async-start | bytes 262144 | tf_op jit(solution)/shard_map/all_to_all | solution.py:238
  21.2 0.0 copy-done.2
  21.2 0.0 copy-done.7
  21.2 0.0 copy-done
  21.2 0.0 copy-done.1
  21.2 2.1 %prepare.1 = (bf16[256,1024]{1,0:T(8,128)(2,1)S(1)}, bf16[256,1024]{1,0:T(8,128)(2,1)S(1)}, bf16[512,512]{1,0:T(8,128)(2,1)S(1)}, bf16[512,512]{1,0:T(8,128)(2,1...) custom-call(bf16[256,512]{1,0:T(8,128)(2,1)S(1)} %copy-done, ...), custom_call_target="tpu_custom_call" | custom-call | tf_op jit(solution)/shard_map/prepare/pallas_call | solution.py:254
  23.3 0.0 copy-start.3
  23.3 0.0 copy-start.5
  23.3 4.4 %all-to-all-done.bc_ref = bf16[16,32,128]{2,1,0:T(8,128)(2,1)S(1)} async-done(((bf16[16,32,128]{2,1,0:T(8,128)(2,1)}), bf16[16,32,128]{2,1,0:T(8,128)(2,1)S(1)}, u32[]{:S(2)}, u32[]{:S(2)}) %all-to-all-start) | async-done | bytes 131104 | tf_op jit(solution)/shard_map/all_to_all | solution.py:238
  27.7 0.4 summary.1
  28.2 0.0 copy-done.3
  28.2 0.0 copy-done.5
  28.2 14.5 %all_to_all.20.got_ref = bf16[32,40,128]{2,1,0:T(8,128)(2,1)S(1)} all-to-all(bf16[32,40,128]{2,1,0:T(8,128)(2,1)S(1)} %summary.1), channel_id=1, replica_groups={{320,336,352,368,384,400,416,432,448,464,480,496,0,16,32,48,64,80,96,11..., dimensions={0} | all-to-all | bytes 655360 | tf_op jit(solution)/shard_map/all_to_all | solution.py:238
  42.6 0.1 scan.1
  42.7 12.0 %all_to_all.21.in_ref = bf16[32,32,128]{2,1,0:T(8,128)(2,1)S(1)} all-to-all(bf16[32,32,128]{2,1,0:T(8,128)(2,1)S(1)} %scan.1), channel_id=1, replica_groups={{320,336,352,368,384,400,416,432,448,464,480,496,0,16,32,48,64,80,96,11..., dimensions={0} | all-to-all | bytes 524288 | tf_op jit(solution)/shard_map/all_to_all | solution.py:238
  54.7 1.2 %sums.1 = bf16[16,32,128]{2,1,0:T(8,128)(2,1)} custom-call(bf16[16,32,128]{2,1,0:T(8,128)(2,1)S(1)} %all-to-all-done.bc_ref, bf16[32,32,128]{2,1,0:T(8,128)(2,1)S(1)} %all_to_all.21.in_ref, bf16[2,256,512]{2,1,0:T(8,128)(2,1)S(1)} %get-tuple-element.23.pr_ref, bf16[256,1024]{1,0:T(8,128)(2,1)S(1)} %get-tuple-element.24.td_ref, ...), custom_call_target="tpu_custom_call" | custom-call | tf_op jit(solution)/shard_map/sums/pallas_call | solution.py:254
  56.0 0.0 copy-start.4
  56.0 0.0 copy-start.6
  56.0 11.6 %all-to-all-start.3 = ((bf16[16,32,128]{2,1,0:T(8,128)(2,1)}), bf16[16,32,128]{2,1,0:T(8,128)(2,1)S(1)}, u32[]{:S(2)}, u32[]{:S(2)}) async-start(bf16[16,32,128]{2,1,0:T(8,128)(2,1)} %sums.1), calls=%async_computation.3 | async-start | bytes 262144 | tf_op jit(solution)/shard_map/all_to_all | solution.py:238
  67.6 0.0 copy-start.8
  67.6 0.0 copy-done.4
  67.6 0.0 copy-done.6
  67.6 0.6 copy-done.8
  68.2 2.5 %finish.1 = (bf16[256,512]{1,0:T(8,128)(2,1)S(1)}, bf16[256,512]{1,0:T(8,128)(2,1)S(1)}) custom-call(bf16[16,32,128]{2,1,0:T(8,128)(2,1)S(1)} %all-to-all-done.bc_ref, bf16[32,32,128]{2,1,0:T(8,128)(2,1)S(1)} %all_to_all.21.in_ref, bf16[24,256]{1,0:T(8,128)(2,1)S(1)} %copy-done.4, bf16[24,256]{1,0:T(8,128)(2,1)S(1)} %copy-done.6, ...), custom_call_target="tpu_custom_call" | custom-call | tf_op jit(solution)/shard_map/finish/pallas_call | solution.py:254
  70.7 0.7 copy.11
  71.4 0.7 copy.12
  72.1 2.1 %all-to-all-done.3.got_ref = bf16[16,32,128]{2,1,0:T(8,128)(2,1)S(1)} async-done(((bf16[16,32,128]{2,1,0:T(8,128)(2,1)}), bf16[16,32,128]{2,1,0:T(8,128)(2,1)S(1)}, u32[]{:S(2)}, u32[]{:S(2)}) %all-to-all-start.3) | async-done | bytes 131104 | tf_op jit(solution)/shard_map/all_to_all | solution.py:238
  74.2 0.6 total.1
  (1 shorter events, 0.0 us)
Async XLA Ops:
  0.6 0.7 copy-start.9
  1.4 19.8 %copy-start.2 = (s32[8,256]{1,0:T(8,128)S(1)}, s32[8,256]{1,0:T(8,128)}, u32[]{:S(2)}) copy-start(s32[8,256]{1,0:T(8,128)} %codes_ref.3) | copy-start | bytes 24580
  1.4 19.8 %copy-start.7 = (f32[8]{0:T(128)S(1)}, f32[8]{0:T(128)}, u32[]{:S(2)}) copy-start(f32[8]{0:T(128)} %rate_ref.3) | copy-start | bytes 100
  1.4 19.8 %copy-start = (bf16[256,512]{1,0:T(8,128)(2,1)S(1)}, bf16[256,512]{1,0:T(8,128)(2,1)}, u32[]{:S(2)}) copy-start(bf16[256,512]{1,0:T(8,128)(2,1)} %x_ref.3) | copy-start | bytes 786436
  1.4 19.8 %copy-start.1 = (bf16[256,512]{1,0:T(8,128)(2,1)S(1)}, bf16[256,512]{1,0:T(8,128)(2,1)}, u32[]{:S(2)}) copy-start(bf16[256,512]{1,0:T(8,128)(2,1)} %dy_ref.3) | copy-start | bytes 786436
  2.1 25.6 %all-to-all-start = ((bf16[16,32,128]{2,1,0:T(8,128)(2,1)}), bf16[16,32,128]{2,1,0:T(8,128)(2,1)S(1)}, u32[]{:S(2)}, u32[]{:S(2)}) async-start(bf16[16,32,128]{2,1,0:T(8,128)(2,1)} %pad_maximum_fusion), calls=%async_computation | async-start | bytes 262144 | tf_op jit(solution)/shard_map/all_to_all | solution.py:238
  23.3 4.9 %copy-start.3 = (bf16[24,256]{1,0:T(8,128)(2,1)}, bf16[24,256]{1,0:T(8,128)(2,1)S(1)}, u32[]{:S(2)}) copy-start(bf16[24,256]{1,0:T(8,128)(2,1)S(1)} %get-tuple-element.19.grow_ref) | copy-start | bytes 36868
  23.3 4.9 %copy-start.5 = (bf16[24,256]{1,0:T(8,128)(2,1)}, bf16[24,256]{1,0:T(8,128)(2,1)S(1)}, u32[]{:S(2)}) copy-start(bf16[24,256]{1,0:T(8,128)(2,1)S(1)} %get-tuple-element.20.dt_ref) | copy-start | bytes 36868
  56.0 11.6 %copy-start.4 = (bf16[24,256]{1,0:T(8,128)(2,1)S(1)}, bf16[24,256]{1,0:T(8,128)(2,1)}, u32[]{:S(2)}) copy-start(bf16[24,256]{1,0:T(8,128)(2,1)} %copy-done.3) | copy-start | bytes 36868
  56.0 11.6 %copy-start.6 = (bf16[24,256]{1,0:T(8,128)(2,1)S(1)}, bf16[24,256]{1,0:T(8,128)(2,1)}, u32[]{:S(2)}) copy-start(bf16[24,256]{1,0:T(8,128)(2,1)} %copy-done.5) | copy-start | bytes 36868
  56.0 18.3 %all-to-all-start.3 = ((bf16[16,32,128]{2,1,0:T(8,128)(2,1)}), bf16[16,32,128]{2,1,0:T(8,128)(2,1)S(1)}, u32[]{:S(2)}, u32[]{:S(2)}) async-start(bf16[16,32,128]{2,1,0:T(8,128)(2,1)} %sums.1), calls=%async_computation.3 | async-start | bytes 262144 | tf_op jit(solution)/shard_map/all_to_all | solution.py:238
  67.6 0.7 copy-start.8

commit v7 on v5

--- a/solution.py
+++ b/solution.py
@@ -11,7 +11,7 @@
 BF = jnp.bfloat16
 F32 = jnp.float32
 HEAD_START = 8
-SEQ_START = 20
+SEQ_START = 21
 
 
 def turned(count, start):

time: 75.2 us -> 74.6 us (level)
  no operation moved by 1% of the time
where the time goes in v7:
time: 74.6 us; the launch traced here: 74.1 us
  starting transfers between devices  30.6 us (41%)
  blocking collectives  26 us (35%)
  Pallas kernels  6.91 us (9%)
  waiting for transfers between devices  6.43 us (9%)
  local copies, waits for them, and re-layouts  2.8 us (4%)
  between operations  0.75 us (1%)
    all_to_all x2, starting transfers between devices, exchange(): return lax.all_to_all(x, axis, 0, 0, tiled=True, axis_index_groups=[order])  30.6 us
    all_to_all x2, blocking collectives, exchange(): return lax.all_to_all(x, axis, 0, 0, tiled=True, axis_index_groups=[order])  26 us
    pallas_call x6, Pallas kernels, kernel(): pl.pallas_call(body, out_shape=shapes, in_specs=specs, out_specs=tuple((p...  6.91 us
    all_to_all x2, waiting for transfers between devices, exchange(): return lax.all_to_all(x, axis, 0, 0, tiled=True, axis_index_groups=[order])  6.43 us
    unnamed x14, local copies, waits for them, and re-layouts  2.09 us
  transfers between devices with their start and end apart: 2, of which 2 were waited for; matrix products, arithmetic and copies ran while one was open for 2% of the time, Pallas kernels for 6%

profile of v7, /device:TPU:1, one launch (start us, length us, event | category | flops | bytes accessed | tf_op | source)
XLA Modules:
  0.0 74.1 jit_solution(10911247644353759392)
XLA Ops:
  0.6 0.0 copy-start.5
  0.6 0.7 broadcast_in_dim.4
  1.3 0.0 copy-done.5
  1.4 0.0 copy-start.2
  1.4 0.0 copy-start.3
  1.4 0.0 copy-start
  1.4 0.0 copy-start.1
  1.4 0.7 pad_maximum_fusion
  2.1 19.1 %all-to-all-start = ((bf16[16,32,128]{2,1,0:T(8,128)(2,1)}), bf16[16,32,128]{2,1,0:T(8,128)(2,1)S(1)}, u32[]{:S(2)}, u32[]{:S(2)}) async-start(bf16[16,32,128]{2,1,0:T(8,128)(2,1)} %pad_maximum_fusion), calls=%async_computation | async-start | bytes 262144 | tf_op jit(solution)/shard_map/all_to_all | solution.py:227
  21.2 0.0 copy-done.2
  21.2 0.0 copy-done.3
  21.2 0.0 copy-done
  21.2 0.0 copy-done.1
  21.2 2.0 %prepare.1 = (bf16[2,256,512]{2,1,0:T(8,128)(2,1)S(1)}, bf16[2,256,512]{2,1,0:T(8,128)(2,1)S(1)}, bf16[4,256,256]{2,1,0:T(8,128)(2,1)S(1)}, bf16[24,256]{1,0:T(8...) custom-call(bf16[256,512]{1,0:T(8,128)(2,1)S(1)} %copy-done, bf16[256,512]{1,0:T(8,128)(2,1)S(1)} %copy-done.1, ...), custom_call_target="tpu_custom_call" | custom-call | tf_op jit(solution)/shard_map/prepare/pallas_call | solution.py:243
  23.2 4.5 %all-to-all-done.bc_ref = bf16[16,32,128]{2,1,0:T(8,128)(2,1)S(1)} async-done(((bf16[16,32,128]{2,1,0:T(8,128)(2,1)}), bf16[16,32,128]{2,1,0:T(8,128)(2,1)S(1)}, u32[]{:S(2)}, u32[]{:S(2)}) %all-to-all-start) | async-done | bytes 131104 | tf_op jit(solution)/shard_map/all_to_all | solution.py:227
  27.7 0.5 summary.1
  28.2 14.2 %all_to_all.20.got_ref = bf16[32,40,128]{2,1,0:T(8,128)(2,1)S(1)} all-to-all(bf16[32,40,128]{2,1,0:T(8,128)(2,1)S(1)} %summary.1), channel_id=1, replica_groups={{336,352,368,384,400,416,432,448,464,480,496,0,16,32,48,64,80,96,112,12..., dimensions={0} | all-to-all | bytes 655360 | tf_op jit(solution)/shard_map/all_to_all | solution.py:227
  42.4 0.1 scan.1
  42.5 11.8 %all_to_all.21.in_ref = bf16[32,32,128]{2,1,0:T(8,128)(2,1)S(1)} all-to-all(bf16[32,32,128]{2,1,0:T(8,128)(2,1)S(1)} %scan.1), channel_id=1, replica_groups={{336,352,368,384,400,416,432,448,464,480,496,0,16,32,48,64,80,96,112,12..., dimensions={0} | all-to-all | bytes 524288 | tf_op jit(solution)/shard_map/all_to_all | solution.py:227
  54.3 1.2 %sums.1 = bf16[16,32,128]{2,1,0:T(8,128)(2,1)} custom-call(bf16[16,32,128]{2,1,0:T(8,128)(2,1)S(1)} %all-to-all-done.bc_ref, bf16[32,32,128]{2,1,0:T(8,128)(2,1)S(1)} %all_to_all.21.in_ref, bf16[4,256,256]{2,1,0:T(8,128)(2,1)S(1)} %get-tuple-element.21.pr_ref, bf16[2,256,512]{2,1,0:T(8,128)(2,1)S(1)} %get-tuple-element.14.td_ref, ...), custom_call_target="tpu_custom_call" | custom-call | tf_op jit(solution)/shard_map/sums/pallas_call | solution.py:243
  55.5 11.5 %all-to-all-start.3 = ((bf16[16,32,128]{2,1,0:T(8,128)(2,1)}), bf16[16,32,128]{2,1,0:T(8,128)(2,1)S(1)}, u32[]{:S(2)}, u32[]{:S(2)}) async-start(bf16[16,32,128]{2,1,0:T(8,128)(2,1)} %sums.1), calls=%async_computation.3 | async-start | bytes 262144 | tf_op jit(solution)/shard_map/all_to_all | solution.py:227
  67.0 0.0 copy-start.4
  67.0 0.6 copy-done.4
  67.6 2.5 %finish.1 = (bf16[256,512]{1,0:T(8,128)(2,1)S(1)}, bf16[256,512]{1,0:T(8,128)(2,1)S(1)}) custom-call(bf16[16,32,128]{2,1,0:T(8,128)(2,1)S(1)} %all-to-all-done.bc_ref, bf16[32,32,128]{2,1,0:T(8,128)(2,1)S(1)} %all_to_all.21.in_ref, bf16[24,256]{1,0:T(8,128)(2,1)S(1)} %get-tuple-element.17.grow_ref, bf16[24,256]{1,0:T(8,128)(2,1)S(1)} %get-tuple-element.18.dt_ref, ...), custom_call_target="tpu_custom_call" | custom-call | tf_op jit(solution)/shard_map/finish/pallas_call | solution.py:243
  70.1 0.7 copy.11
  70.8 0.7 copy.12
  71.5 2.0 %all-to-all-done.3.got_ref = bf16[16,32,128]{2,1,0:T(8,128)(2,1)S(1)} async-done(((bf16[16,32,128]{2,1,0:T(8,128)(2,1)}), bf16[16,32,128]{2,1,0:T(8,128)(2,1)S(1)}, u32[]{:S(2)}, u32[]{:S(2)}) %all-to-all-start.3) | async-done | bytes 131104 | tf_op jit(solution)/shard_map/all_to_all | solution.py:227
  73.5 0.6 total.1
  (1 shorter events, 0.0 us)
Async XLA Ops:
  0.6 0.7 copy-start.5
  1.4 19.8 %copy-start.2 = (s32[8,256]{1,0:T(8,128)S(1)}, s32[8,256]{1,0:T(8,128)}, u32[]{:S(2)}) copy-start(s32[8,256]{1,0:T(8,128)} %codes_ref.3) | copy-start | bytes 24580
  1.4 19.8 %copy-start.3 = (f32[8]{0:T(128)S(1)}, f32[8]{0:T(128)}, u32[]{:S(2)}) copy-start(f32[8]{0:T(128)} %rate_ref.3) | copy-start | bytes 100
  1.4 19.8 %copy-start = (bf16[256,512]{1,0:T(8,128)(2,1)S(1)}, bf16[256,512]{1,0:T(8,128)(2,1)}, u32[]{:S(2)}) copy-start(bf16[256,512]{1,0:T(8,128)(2,1)} %x_ref.3) | copy-start | bytes 786436
  1.4 19.8 %copy-start.1 = (bf16[256,512]{1,0:T(8,128)(2,1)S(1)}, bf16[256,512]{1,0:T(8,128)(2,1)}, u32[]{:S(2)}) copy-start(bf16[256,512]{1,0:T(8,128)(2,1)} %dy_ref.3) | copy-start | bytes 786436
  2.1 25.6 %all-to-all-start = ((bf16[16,32,128]{2,1,0:T(8,128)(2,1)}), bf16[16,32,128]{2,1,0:T(8,128)(2,1)S(1)}, u32[]{:S(2)}, u32[]{:S(2)}) async-start(bf16[16,32,128]{2,1,0:T(8,128)(2,1)} %pad_maximum_fusion), calls=%async_computation | async-start | bytes 262144 | tf_op jit(solution)/shard_map/all_to_all | solution.py:227
  55.5 18.0 %all-to-all-start.3 = ((bf16[16,32,128]{2,1,0:T(8,128)(2,1)}), bf16[16,32,128]{2,1,0:T(8,128)(2,1)S(1)}, u32[]{:S(2)}, u32[]{:S(2)}) async-start(bf16[16,32,128]{2,1,0:T(8,128)(2,1)} %sums.1), calls=%async_computation.3 | async-start | bytes 262144 | tf_op jit(solution)/shard_map/all_to_all | solution.py:227
  67.0 0.7 copy-start.4
